TPU v7x, 512 devices: a whole 4x8x8 slice. The times are simulated.
512 devices in a mesh: sec: 16 (over z_hi, x), row: 32 (over y, z_lo, core).
Axes of the slice: x: 4, y: 8, z: 8 (z_hi: 4, z_lo: 2; z = z_hi * 2 + z_lo), core: 2. Of those that a mesh axis runs over, the one named last changes fastest.
Arguments:
- source: bfloat16 [16, 8192, 2048], P('sec', 'row'), may hold values from -120 to 120, as said below
- routes: int32 [16, 1024], P('sec', 'row'), may hold values from 0 to 1023, as said below
- offsets: float32 [16, 2, 1024], P('sec', None, 'row'), may hold values from 0 to 1
Outputs:
- rendered: float32 [16, 8192, 2048], P('sec', 'row')
- flows: float32 [16, 2, 128, 32], P('sec', None, 'row')
Inputs may be any that keep to these rules, and one draw needn't show every extreme that they name: `source`: magnitudes vary from row to row and column to column. `routes`: the 32 output blocks of one device's strip read at most 2 source blocks from the strip of any one device of the same section, and exactly 2 from some device.
All inputs are finite; a program needn't handle non-finite values.
Results may differ from a plain program's by a relative error of at most 0.0003.
Values may be sent and summed in bfloat16 or wider, within the bound.
No kernel may reach another device: no remote copies, remote signals or barrier semaphores. Data moves between devices by JAX's collectives and lax.ppermute only.
A program may use at most 64 MiB of HBM per device.

v0:
```python
import jax
import jax.numpy as jnp
from jax import lax
from jax.sharding import PartitionSpec as P

peak_floor = 64.0
tiny_value = 1e-06


def in_order(pieces, dim):
    pieces = jnp.moveaxis(pieces, 0, dim)
    shape = pieces.shape
    return pieces.reshape(*shape[:dim], shape[dim] * shape[dim + 1], *shape[dim + 2 :])


def copy_for_each(value, axis):
    copies = jnp.broadcast_to(value, (lax.axis_size(axis), *value.shape))
    return lax.all_to_all(copies, axis, split_axis=0, concat_axis=0, tiled=True)


def gather_directly(value, axis, dim):
    return in_order(copy_for_each(value, axis), dim)


def shifted(value, axis, steps):
    count = lax.axis_size(axis)
    first, last = (max(0, -steps), min(count, count - steps))
    return lax.ppermute(value, axis, [(source, source + steps) for source in range(first, last)])


def bilinear(square, downward, across):
    step_right = jnp.concatenate([square[:, :, 1:], square[:, :, -1:]], 2)
    step_down = jnp.concatenate([square[:, 1:], square[:, -1:]], 1)
    step_both = jnp.concatenate([step_right[:, 1:], step_right[:, -1:]], 1)
    downward = downward[:, None, None]
    across = across[:, None, None]
    upper_row = (1.0 - across) * square + across * step_right
    lower_row = (1.0 - across) * step_down + across * step_both
    return (1.0 - downward) * upper_row + downward * lower_row


def to_blocks(section_strip):
    row_total, col_total = section_strip.shape
    return (
        section_strip.reshape(row_total // 128, 128, col_total // 128, 128)
        .transpose(0, 2, 1, 3)
        .reshape(-1, 128, 128)
    )


def from_blocks(tiles, row_total, col_total):
    return (
        tiles.reshape(row_total // 128, col_total // 128, 128, 128)
        .transpose(0, 2, 1, 3)
        .reshape(row_total, col_total)
    )


def parabola(nearby):
    profile_down = (nearby[..., 0] + 2.0 * nearby[..., 1] + nearby[..., 2]) * 0.25
    profile_across = (nearby[..., 0, :] + 2.0 * nearby[..., 1, :] + nearby[..., 2, :]) * 0.25
    curve_down = jnp.maximum(
        2.0 * profile_down[..., 1] - profile_down[..., 0] - profile_down[..., 2], peak_floor
    )
    curve_across = jnp.maximum(
        2.0 * profile_across[..., 1] - profile_across[..., 0] - profile_across[..., 2], peak_floor
    )
    flow_down = (profile_down[..., 2] - profile_down[..., 0]) / (2.0 * curve_down)
    flow_across = (profile_across[..., 2] - profile_across[..., 0]) / (2.0 * curve_across)
    return jnp.stack([flow_down, flow_across], 0)


def flows_of(first, second):
    row_total, col_total = first.shape
    exact = lax.Precision.HIGHEST
    counter = jnp.arange(64, dtype=jnp.int32)
    angles = 2.0 * jnp.pi / 64.0 * (counter[:, None] * counter[None, :] % 64).astype(jnp.float32)
    cosine = jnp.cos(angles)
    sine = jnp.sin(angles)
    row_table = jnp.concatenate([cosine, -sine], 1)
    shifts = jnp.array([-1, 0, 1], dtype=jnp.int32)
    phase_index = (
        counter[:, None, None, None] * shifts[None, None, :, None]
        + counter[None, :, None, None] * shifts[None, None, None, :]
    ) % 64
    phases = 2.0 * jnp.pi / 64.0 * phase_index.astype(jnp.float32).reshape(4096, 9)
    back_cos = jnp.cos(phases)
    back_sin = jnp.sin(phases)

    def patchify(band):
        padded = jnp.concatenate([jnp.zeros((64, 32), jnp.float32), band[:, : col_total - 32]], 1)
        tiles = padded.reshape(64, col_total // 64, 64).transpose(1, 0, 2)
        centred = tiles - jnp.mean(tiles, axis=(1, 2), keepdims=True)
        return centred / jnp.sqrt(
            jnp.mean(centred * centred, axis=(1, 2), keepdims=True) + tiny_value
        )

    def spectrum(tiles):
        halfway = jnp.einsum("nyx,xl->nyl", tiles, row_table, precision=exact)
        swapped = jnp.concatenate([halfway[:, :, 64:], -halfway[:, :, :64]], 2)
        return jnp.einsum("ky,nyl->nkl", cosine, halfway, precision=exact) + jnp.einsum(
            "ky,nyl->nkl", sine, swapped, precision=exact
        )

    def one_band(bands):
        spec_first = spectrum(patchify(bands[0]))
        spec_second = spectrum(patchify(bands[1]))
        first_real, first_imag = (spec_first[:, :, :64], spec_first[:, :, 64:])
        second_real, second_imag = (spec_second[:, :, :64], spec_second[:, :, 64:])
        cross_real = (first_real * second_real + first_imag * second_imag).reshape(-1, 4096)
        cross_imag = (first_real * second_imag - first_imag * second_real).reshape(-1, 4096)
        nearby = (
            jnp.dot(cross_real, back_cos, precision=exact)
            - jnp.dot(cross_imag, back_sin, precision=exact)
        ) / 4096.0
        return parabola(nearby.reshape(-1, 3, 3))

    bands = (
        first.reshape(row_total // 64, 64, col_total),
        second.reshape(row_total // 64, 64, col_total),
    )
    return lax.map(one_band, bands).transpose(1, 0, 2)


def on_device(source, routes, offsets):
    section_strip = source[0]
    row_total, col_total = section_strip.shape
    local_blocks = to_blocks(section_strip)
    block_count = local_blocks.shape[0]
    row_count = lax.axis_size("row")
    slot_count = max(2, 2 * block_count // row_count)
    my_index = lax.axis_index("row")
    own_route = routes[0]
    own_offsets = offsets[0]
    every_route = gather_directly(own_route, "row", 0).reshape(row_count, block_count)
    owners = every_route // block_count
    spot_index = every_route % block_count
    earlier = jnp.arange(block_count)[:, None] > jnp.arange(block_count)[None, :]
    matching = owners[:, :, None] == owners[:, None, :]
    ranking = jnp.sum((matching & earlier[None]).astype(jnp.int32), axis=2)
    is_mine = owners == my_index
    selected = is_mine[:, None, :] & (ranking[:, None, :] == jnp.arange(slot_count)[None, :, None])
    picked = jnp.sum(jnp.where(selected, spot_index[:, None, :], 0), axis=2).reshape(-1)
    own_rank = lax.dynamic_index_in_dim(ranking, my_index, 0, keepdims=False)
    slot_of = own_route // block_count * slot_count + own_rank
    outgoing = local_blocks[picked]
    arrived = lax.all_to_all(outgoing, "row", split_axis=0, concat_axis=0, tiled=True)
    chosen = arrived[slot_of].astype(jnp.float32)
    rendered_tiles = bilinear(chosen, own_offsets[0], own_offsets[1])
    rendered_strip = from_blocks(rendered_tiles, row_total, col_total)
    upper_rim = shifted(rendered_strip[row_total - 32 :], "row", 1)
    own_used = jnp.concatenate([upper_rim, rendered_strip[: row_total - 32]], 0)
    partner = shifted(own_used, "sec", -1)
    flows = flows_of(own_used, partner)
    return (rendered_strip[None], flows[None])


def solution(mesh):
    placed = (P("sec", "row", None), P("sec", "row"), P("sec", None, "row"))
    return jax.shard_map(
        on_device,
        mesh=mesh,
        in_specs=placed,
        out_specs=(P("sec", "row", None), P("sec", None, "row", None)),
        check_vma=False,
    )
```

profile of v0, /device:TPU:143, one launch (start us, length us, event | category | flops | bytes accessed | tf_op | source)
XLA Modules:
  0.0 264.5 jit_solution(12761635804379813629)
XLA Ops:
  0.6 1.3 broadcast_in_dim.23
  1.9 9.8 %all-to-all-start = ((s32[32,1,32]{2,1,0:T(1,128)}), s32[32,1,32]{2,1,0:T(1,128)S(1)}, u32[]{:S(2)}, u32[]{:S(2)}) async-start(s32[32,1,32]{2,1,0:T(1,128)} %broadcast_in_dim.23), calls=%async_computation | async-start | bytes 32768 | tf_op jit(solution)/shard_map/all_to_all | solution.py:18
  11.7 1.5 copy.83
  13.6 4.8 %all-to-all-done = s32[32,1,32]{2,1,0:T(1,128)S(1)} async-done(((s32[32,1,32]{2,1,0:T(1,128)}), s32[32,1,32]{2,1,0:T(1,128)S(1)}, u32[]{:S(2)}, u32[]{:S(2)}) %all-to-all-start) | async-done | bytes 4128 | tf_op jit(solution)/shard_map/all_to_all | solution.py:18
  19.7 2.1 gather_fusion
  21.8 5.5 %all-to-all-start.1 = ((bf16[64,128,128]{2,1,0:T(8,128)(2,1)}), bf16[64,128,128]{2,1,0:T(8,128)(2,1)S(1)}, u32[]{:S(2)}, u32[]{:S(2)}) async-start(bf16[64,128,128]{2,1,0:T(8,128)(2,1)} %gather_fusion), calls=%async_computation.1 | async-start | bytes 4194304 | tf_op jit(solution)/shard_map/all_to_all | solution.py:147
  27.5 49.8 %all-to-all-done.1 = bf16[64,128,128]{2,1,0:T(8,128)(2,1)S(1)} async-done(((bf16[64,128,128]{2,1,0:T(8,128)(2,1)}), bf16[64,128,128]{2,1,0:T(8,128)(2,1)S(1)}, u32[]{:S(2)}, u32[]{:S(2)}) %all-to-all-start.1) | async-done | bytes 2097184 | tf_op jit(solution)/shard_map/all_to_all | solution.py:147
  80.2 1.7 fusion.89
  81.9 1.2 copy.74
  84.1 4.0 %collective-permute-start = (f32[32,2048]{1,0:T(8,128)S(1)}, f32[32,2048]{1,0:T(8,128)S(1)}, u32[]{:S(2)}, u32[]{:S(2)}) collective-permute-start(f32[32,2048]{1,0:T(8,128)S(1)} %slice.204), channel_id=1, source_target_pairs={{0,1},{1,2},{2,3},{3,4},{4,5},{5,6},{6,7},{7,8},{8,9},{9,10},{10,1... | collective-permute-start | bytes 786440 | tf_op jit(solution)/shard_map/ppermute | solution.py:28
  88.2 3.1 %collective-permute-done = f32[32,2048]{1,0:T(8,128)S(1)} collective-permute-done((f32[32,2048]{1,0:T(8,128)S(1)}, f32[32,2048]{1,0:T(8,128)S(1)}, u32[]{:S(2)}, u32[]{:S(2)}) %collective-permute-start) | collective-permute-done | bytes 262176 | tf_op jit(solution)/shard_map/ppermute | solution.py:28
  91.3 1.5 pad_maximum_fusion.1
  92.8 2.4 collective-permute-start.1
  95.6 1.5 broadcast_in_dim_reshape.3
  97.1 94.5 %collective-permute-done.1 = f32[256,2048]{1,0:T(8,128)} collective-permute-done((f32[256,2048]{1,0:T(8,128)}, f32[256,2048]{1,0:T(8,128)}, u32[]{:S(2)}, u32[]{:S(2)}) %collective-permute-start.1) | collective-permute-done | bytes 2097184 | tf_op jit(solution)/shard_map/ppermute | solution.py:28
  191.6 72.3 %while.13 = (s32[]{:T(128)}, f32[4,2,32]{2,0,1:T(4,128)S(1)}, f32[4,64,2048]{2,1,0:T(8,128)}, f32[64,128]{1,0:T(8,128)S(1)}, f32[4,64,2048]{2,1,0:T(8,128)}, /*i...) while((s32[]{:T(128)}, f32[4,2,32]{2,0,1:T(4,128)S(1)}, ...), condition=%wide.region_9.10_spmd.clone.clone.clone, body=%wide.region_2.9_spmd.clone.clone.clone.sunk | while | flops 1241167616 | bytes 34421228 | solution.py:122
  191.6 1.3 dynamic-slice_bitcast_fusion.3
  194.3 1.7 fusion.164
  196.4 1.1 fusion.165
  197.6 1.4 fusion.167
  200.3 1.7 fusion.160
  203.6 1.4 fusion.163
  206.2 1.5 fusion.168
  208.0 1.5 fusion.169
  209.7 1.3 dynamic-slice_bitcast_fusion.3
  212.4 1.7 fusion.164
  215.6 1.4 fusion.167
  218.4 1.7 fusion.160
  220.5 1.1 fusion.161
  221.7 1.4 fusion.163
  224.3 1.5 fusion.168
  226.1 1.5 fusion.169
  227.7 1.3 dynamic-slice_bitcast_fusion.3
  230.4 1.7 fusion.164
  233.7 1.4 fusion.167
  236.5 1.7 fusion.160
  238.6 1.1 fusion.161
  239.7 1.4 fusion.163
  242.3 1.5 fusion.168
  244.2 1.5 fusion.169
  245.8 1.3 dynamic-slice_bitcast_fusion.3
  248.5 1.7 fusion.164
  251.8 1.4 fusion.167
  254.6 1.7 fusion.160
  256.6 1.1 fusion.161
  257.8 1.4 fusion.163
  260.4 1.5 fusion.168
  262.2 1.5 fusion.169
  (169 shorter events, 32.1 us)
Async XLA Ops:
  1.9 16.6 %all-to-all-start = ((s32[32,1,32]{2,1,0:T(1,128)}), s32[32,1,32]{2,1,0:T(1,128)S(1)}, u32[]{:S(2)}, u32[]{:S(2)}) async-start(s32[32,1,32]{2,1,0:T(1,128)} %broadcast_in_dim.23), calls=%async_computation | async-start | bytes 32768 | tf_op jit(solution)/shard_map/all_to_all | solution.py:18
  21.8 5.5 %copy-start.1 = (f32[1,2,32]{2,1,0:T(2,128)S(1)}, f32[1,2,32]{2,1,0:T(2,128)}, u32[]{:S(2)}) copy-start(f32[1,2,32]{2,1,0:T(2,128)} %param.8) | copy-start | bytes 772
  21.8 5.7 %copy-start = (s32[1,32]{1,0:T(1,128)S(1)}, s32[1,32]{1,0:T(1,128)}, u32[]{:S(2)}) copy-start(s32[1,32]{1,0:T(1,128)} %param.7) | copy-start | bytes 388
  21.8 55.5 %all-to-all-start.1 = ((bf16[64,128,128]{2,1,0:T(8,128)(2,1)}), bf16[64,128,128]{2,1,0:T(8,128)(2,1)S(1)}, u32[]{:S(2)}, u32[]{:S(2)}) async-start(bf16[64,128,128]{2,1,0:T(8,128)(2,1)} %gather_fusion), calls=%async_computation.1 | async-start | bytes 4194304 | tf_op jit(solution)/shard_map/all_to_all | solution.py:147
  84.1 7.3 %collective-permute-start = (f32[32,2048]{1,0:T(8,128)S(1)}, f32[32,2048]{1,0:T(8,128)S(1)}, u32[]{:S(2)}, u32[]{:S(2)}) collective-permute-start(f32[32,2048]{1,0:T(8,128)S(1)} %slice.204), channel_id=1, source_target_pairs={{0,1},{1,2},{2,3},{3,4},{4,5},{5,6},{6,7},{7,8},{8,9},{9,10},{10,1... | collective-permute-start | bytes 786440 | tf_op jit(solution)/shard_map/ppermute | solution.py:28
  88.2 7.3 %copy-start.2 = (s32[3]{0:T(128)S(1)}, s32[3]{0:T(128)}, u32[]{:S(2)}) copy-start(s32[3]{0:T(128)} %constant.113.clone) | copy-start | bytes 40
  92.8 98.8 %collective-permute-start.1 = (f32[256,2048]{1,0:T(8,128)}, f32[256,2048]{1,0:T(8,128)}, u32[]{:S(2)}, u32[]{:S(2)}) collective-permute-start(f32[256,2048]{1,0:T(8,128)} %pad_maximum_fusion.1), channel_id=1, source_target_pairs={{32,0},{64,32},{96,64},{128,96},{160,128},{192,160},{224,192},{256... | collective-permute-start | bytes 6291464 | tf_op jit(solution)/shard_map/ppermute | solution.py:28
  263.9 0.6 copy-start.3
where the time goes:
time: 265 us; the launch traced here: 264 us
  waiting for transfers between devices  152 us (57%)
  matrix products  45.5 us (17%)
  local copies, waits for them, and re-layouts  24.5 us (9%)
  starting transfers between devices  21.7 us (8%)
  other arithmetic  19 us (7%)
    ppermute x2, waiting for transfers between devices, shifted(): lax.ppermute(value, axis, [(source, source + steps) for source in range(f...  97.6 us
    all_to_all x1, waiting for transfers between devices, on_device(): lax.all_to_all(outgoing, 'row', split_axis=0, concat_axis=0, tiled=True)  49.8 us
    dot_general x8, matrix products, spectrum(): halfway = jnp.einsum('nyx,xl->nyl', tiles, row_table, precision=exact)  13.5 us
    dot_general x8, matrix products, spectrum(): jnp.einsum('ky,nyl->nkl', sine, swapped, precision=exact)  11 us
    all_to_all x1, starting transfers between devices, copy_for_each(): return lax.all_to_all(copies, axis, split_axis=0, concat_axis=0, tiled=True)  9.79 us
    dot_general x8, matrix products, spectrum(): jnp.einsum('ky,nyl->nkl', cosine, halfway, precision=exact)  9.19 us
    ppermute x2, starting transfers between devices, shifted(): lax.ppermute(value, axis, [(source, source + steps) for source in range(f...  6.4 us
    dot_general x4, matrix products, one_band(): jnp.dot(cross_imag, back_sin, precision=exact)  5.89 us
  transfers between devices with their start and end apart: 4, of which 4 were waited for; matrix products, arithmetic and copies ran while one was open for 2% of the time, Pallas kernels for 0%

commit v1 on v0

v1 whole, which is shorter than its diff:
```python
import functools

import jax
import jax.numpy as jnp
from jax import lax
from jax.experimental import pallas as pl
from jax.experimental.pallas import tpu as pltpu
from jax.sharding import PartitionSpec as P


peak_floor = 64.0
tiny_value = 1e-06
BLOCK = 128
PATCH = 64
SPLIT = 32
VMEM = pltpu.VMEM
SMEM = pltpu.SMEM
F32 = jnp.float32
BF16 = jnp.bfloat16


def spec(space):
    return pl.BlockSpec(memory_space=space)


def shape(dims, dtype):
    return jax.ShapeDtypeStruct(dims, dtype)


def params(limit=14 << 20):
    return pltpu.CompilerParams(vmem_limit_bytes=limit)


def cut_blocks(strip_ref, out_ref):
    wide = strip_ref.shape[1] // BLOCK
    for i in range(strip_ref.shape[0] // BLOCK):
        for k in range(wide):
            out_ref[i * wide + k] = strip_ref[i * BLOCK : (i + 1) * BLOCK, k * BLOCK : (k + 1) * BLOCK]


def blocks_of(strip):
    rows, cols = strip.shape
    return pl.pallas_call(
        cut_blocks,
        out_shape=shape((rows // BLOCK * (cols // BLOCK), BLOCK, BLOCK), strip.dtype),
        in_specs=[spec(VMEM)],
        out_specs=spec(VMEM),
        compiler_params=params(),
        cost_estimate=pl.CostEstimate(flops=0, bytes_accessed=2_000_000, transcendentals=0),
    )(strip)


def pack_requested(row_from, rows, picked_ref, blocks_ref, out_ref, sem):
    def one(i, carry):
        spot = picked_ref[i // 2, 0, i % 2]
        pltpu.make_async_copy(blocks_ref.at[spot, pl.ds(row_from, rows), :], out_ref.at[i], sem).start()
        return carry

    lax.fori_loop(0, out_ref.shape[0], one, 0, unroll=8)
    pltpu.make_async_copy(out_ref, out_ref, sem).wait()


def requested(picked, blocks, row_from, rows):
    slots = 2 * picked.shape[0]
    return pl.pallas_call(
        functools.partial(pack_requested, row_from, rows),
        out_shape=shape((slots, rows, BLOCK), blocks.dtype),
        in_specs=[spec(SMEM), spec(VMEM)],
        out_specs=spec(pl.ANY),
        scratch_shapes=[pltpu.SemaphoreType.DMA],
        compiler_params=params(55_000_000),
    )(picked, blocks)


def pack_for_sections(slot_ref, deep_ref, middle_ref, top_ref, bottom_ref, first_ref, next_ref):
    half = bottom_ref.shape[0]

    def one(b, carry):
        s = slot_ref[b]
        middle_ref[b] = deep_ref[s, pl.ds(0, 64), :]
        first_ref[pl.ds(b, 1), :] = deep_ref[s, pl.ds(0, 16), :].astype(F32)[0:1]
        next_ref[pl.ds(b, 1), :] = deep_ref[s, pl.ds(64, 16), :].astype(F32)[0:1]
        return carry

    lax.fori_loop(0, 2 * half, one, 0, unroll=4)

    def tails(b, carry):
        top_ref[b] = deep_ref[slot_ref[b], pl.ds(64, 32), :]
        bottom_ref[b] = deep_ref[slot_ref[half + b], pl.ds(64, 32), :]
        return carry

    lax.fori_loop(0, half, tails, 0, unroll=4)
    middle_ref[2 * half, pl.ds(0, 32), :] = next_ref[...].astype(BF16)
    middle_ref[2 * half, pl.ds(32, 32), :] = jnp.zeros((32, BLOCK), BF16)
    top_ref[half] = first_ref[...].astype(BF16)


def section_parts(slot, deep):
    count = slot.shape[0]
    half = count // 2
    return pl.pallas_call(
        pack_for_sections,
        out_shape=(
            shape((count + 1, 64, BLOCK), BF16),
            shape((half + 1, 32, BLOCK), BF16),
            shape((half, 32, BLOCK), BF16),
        ),
        in_specs=[spec(SMEM), spec(VMEM)],
        out_specs=(spec(VMEM), spec(VMEM), spec(VMEM)),
        scratch_shapes=[VMEM((count, BLOCK), F32), VMEM((count, BLOCK), F32)],
        compiler_params=params(),
    )(slot, deep)


def pack_shallow(slot_ref, shallow_ref, out_ref):
    def one(b, carry):
        out_ref[b] = shallow_ref[slot_ref[b]]
        return carry

    lax.fori_loop(0, out_ref.shape[0], one, 0, unroll=4)


def shallow_part(slot, shallow):
    return pl.pallas_call(
        pack_shallow,
        out_shape=shape((slot.shape[0], *shallow.shape[1:]), BF16),
        in_specs=[spec(SMEM), spec(VMEM)],
        out_specs=spec(VMEM),
        compiler_params=params(),
    )(slot, shallow)


def mixed_across(square, across):
    lane = lax.broadcasted_iota(jnp.int32, square.shape, 1)
    moved = jnp.where(lane == BLOCK - 1, square, pltpu.roll(square, BLOCK - 1, 1))
    return (1.0 - across) * square + across * moved


def render_rows(square, following, downward, across):
    rows = square.shape[0]
    mixed = mixed_across(square, across)
    below = mixed if following is None else mixed_across(following, across)
    row = lax.broadcasted_iota(jnp.int32, square.shape, 0)
    moved = jnp.where(row == rows - 1, below, pltpu.roll(mixed, rows - 1, 0))
    return (1.0 - downward) * mixed + downward * moved


def joined(made, carried):
    lane = lax.broadcasted_iota(jnp.int32, made.shape, 1)
    return jnp.where(lane < BLOCK - PATCH // 2, made, carried)


def same_patch():
    half = PATCH // 2
    one = lax.broadcasted_iota(jnp.int32, (BLOCK, BLOCK), 0)
    two = lax.broadcasted_iota(jnp.int32, (BLOCK, BLOCK), 1)
    return ((((one + half) // PATCH) % 2) == (((two + half) // PATCH) % 2)).astype(F32)


def per_patch(values):
    return jnp.dot(values, same_patch(), precision=lax.Precision.HIGHEST)


def filter_tiles(tall_ref, sums_ref, soft_ref, step_ref, bend_ref, power_ref):
    half = PATCH // 2
    sums_ref[...] = per_patch(sums_ref[...]) / float(PATCH * PATCH)

    def filtered(t, carry):
        b = tall_ref[t] - sums_ref[pl.ds(t, 1), :]
        lane = lax.broadcasted_iota(jnp.int32, b.shape, 1) % PATCH
        swapped = pltpu.roll(b, PATCH, 1)
        after = pltpu.roll(jnp.where(lane == half, swapped, b), BLOCK - 1, 1)
        before = pltpu.roll(jnp.where(lane == half - 1, swapped, b), 1, 1)
        pair = after + before
        twice = b + b
        soft_ref[t] = 0.25 * (twice + pair)
        step_ref[t] = after - before
        bend_ref[t] = twice - pair
        power_ref[pl.ds(t, 1), :] = jnp.sum(b * b, axis=0, keepdims=True)
        return carry

    lax.fori_loop(0, tall_ref.shape[0], filtered, 0, unroll=2)
    power_ref[...] = per_patch(power_ref[...])


def own_rim(offset_ref, rim_ref, out_ref):
    wide = rim_ref.shape[0]

    def one(k, carry):
        out_ref[k] = render_rows(rim_ref[k].astype(F32), None, offset_ref[0, wide + k], offset_ref[1, wide + k])
        return carry

    lax.fori_loop(0, wide, one, 0, unroll=2)


def render_rim(offsets, rim):
    return pl.pallas_call(
        own_rim,
        out_shape=shape(rim.shape, F32),
        in_specs=[spec(SMEM), spec(VMEM)],
        out_specs=spec(VMEM),
        compiler_params=params(),
        cost_estimate=pl.CostEstimate(flops=600_000, bytes_accessed=400_000, transcendentals=0),
    )(offsets, rim)


def own_strip(slot_ref, offset_ref, deep_ref, shallow_ref, rim_ref, image_ref, soft_ref, step_ref, bend_ref, power_ref, tall_ref, sums_ref):
    wide = rim_ref.shape[0]
    tiles = 2 * wide
    half = PATCH // 2
    for strip in range(2):

        def one(k, carried, strip=strip):
            b = strip * wide + k
            s = slot_ref[b]
            square = jnp.concatenate([shallow_ref[s], deep_ref[s]], 0).astype(F32)
            made = render_rows(square, None, offset_ref[0, b], offset_ref[1, b])
            image_ref[pl.ds(strip * BLOCK, BLOCK), pl.ds(pl.multiple_of(k * BLOCK, BLOCK), BLOCK)] = made
            tile = joined(made, carried)
            middle = tile[half : half + PATCH]
            tall_ref[b] = middle
            sums_ref[pl.ds(b, 1), :] = jnp.sum(middle, axis=0, keepdims=True)
            tall_ref[tiles + b, pl.ds(half, half), :] = tile[:half]
            low = jnp.sum(tile[:half], axis=0, keepdims=True)
            if strip == 0:
                tall_ref[tiles + wide + b, pl.ds(0, half), :] = tile[half + PATCH :]
                sums_ref[pl.ds(tiles + wide + b, 1), :] = jnp.sum(tile[half + PATCH :], axis=0, keepdims=True)
                sums_ref[pl.ds(tiles + b, 1), :] = low
            else:
                sums_ref[pl.ds(tiles + b, 1), :] += low
            return made

        lax.fori_loop(0, wide, one, jnp.zeros((BLOCK, BLOCK), F32))

    def rim_one(k, carried):
        made = rim_ref[k]
        tile = joined(made, carried)
        tall_ref[tiles + k, pl.ds(0, half), :] = tile
        sums_ref[pl.ds(tiles + k, 1), :] += jnp.sum(tile, axis=0, keepdims=True)
        return made

    lax.fori_loop(0, wide, rim_one, jnp.zeros((half, BLOCK), F32), unroll=2)
    filter_tiles(tall_ref, sums_ref, soft_ref, step_ref, bend_ref, power_ref)


def render_strip(slot, offsets, deep, shallow, rim, rows, cols):
    tiles = 2 * slot.shape[0]
    tile = shape((tiles, PATCH, BLOCK), F32)
    return pl.pallas_call(
        own_strip,
        out_shape=(shape((rows, cols), F32), tile, tile, tile, shape((tiles, BLOCK), F32)),
        in_specs=[spec(SMEM)] * 2 + [spec(VMEM)] * 3,
        out_specs=(spec(VMEM),) * 5,
        scratch_shapes=[VMEM((tiles, PATCH, BLOCK), F32), VMEM((tiles, BLOCK), F32)],
        compiler_params=params(),
        cost_estimate=pl.CostEstimate(flops=12_000_000, bytes_accessed=3_000_000, transcendentals=0),
    )(slot, offsets, deep, shallow, rim)


PAD = 8


def keep_tile(tile, t, tiles_ref, sums_ref):
    tiles_ref[t, pl.ds(PAD, PATCH), :] = tile
    tiles_ref[t, pl.ds(PAD - 1, 1), :] = tile[PATCH - 1 :]
    tiles_ref[t, pl.ds(PAD + PATCH, 1), :] = tile[:1]
    sums_ref[pl.ds(t, 1), :] = jnp.sum(tile, axis=0, keepdims=True)


def correlate(own_is_first, base, tiles_ref, sums_ref, acc_ref, soft_ref, step_ref, bend_ref, power_ref):
    area = float(PATCH * PATCH)
    tiles = sums_ref.shape[0]
    sums_ref[...] = per_patch(sums_ref[...]) / area

    def one(t, carry):
        mean = sums_ref[pl.ds(t, 1), :]
        o = tiles_ref[t, pl.ds(PAD, PATCH), :]
        after = tiles_ref[t, pl.ds(PAD + 1, PATCH), :]
        before = tiles_ref[t, pl.ds(PAD - 1, PATCH), :]
        pair = after + before
        twice = o + o
        soft = 0.25 * (twice + pair) - mean
        step = after - before
        bend = twice - pair
        flat = o - mean
        own_soft = soft_ref[base + t]
        products = (flat * flat, own_soft * step, own_soft * bend, step_ref[base + t] * soft, bend_ref[base + t] * soft)
        for q, product in enumerate(products):
            acc_ref[pl.ds(q * tiles + t, 1), :] = jnp.sum(product, axis=0, keepdims=True)
        return carry

    lax.fori_loop(0, tiles, one, 0, unroll=2)
    totals = per_patch(acc_ref[...])
    part = [totals[q * tiles : (q + 1) * tiles] for q in range(5)]
    scale = 1.0 / (jnp.sqrt(part[0] / area + tiny_value) * jnp.sqrt(power_ref[pl.ds(base, tiles), :] / area + tiny_value))
    signs = (1.0, -1.0) if own_is_first else (-1.0, 1.0)
    down = signs[0] * part[1] * scale / (2.0 * jnp.maximum(part[2] * scale, peak_floor))
    across = signs[1] * part[3] * scale / (2.0 * jnp.maximum(part[4] * scale, peak_floor))
    return down, across


def patch_row(values):
    lane = lax.broadcasted_iota(jnp.int32, values.shape, 1)
    row = lax.broadcasted_iota(jnp.int32, values.shape, 0)
    chosen = jnp.where(lane % 2 == 0, values, pltpu.roll(values, PATCH, 1))
    return jnp.sum(jnp.where(lane // 2 == row, chosen, 0.0), axis=0, keepdims=True)[:, : 2 * values.shape[0]]


def flow_scratch(tiles):
    return [
        VMEM((tiles, PATCH + 2 * PAD, BLOCK), F32),
        VMEM((tiles, BLOCK), F32),
        VMEM((5 * tiles, BLOCK), F32),
        VMEM((tiles, BLOCK), F32),
    ]


def flow_middle(offset_ref, other_ref, soft_ref, step_ref, bend_ref, power_ref, out_ref, tiles_ref, sums_ref, acc_ref, next_ref):
    tiles = sums_ref.shape[0]
    wide = tiles // 2
    next_ref[...] = other_ref[tiles, pl.ds(0, tiles), :].astype(F32)
    for strip in range(2):

        def one(k, carried, strip=strip):
            t = strip * wide + k
            made = render_rows(other_ref[t].astype(F32), next_ref[pl.ds(t, 1), :], offset_ref[0, t], offset_ref[1, t])
            keep_tile(joined(made, carried), t, tiles_ref, sums_ref)
            return made

        lax.fori_loop(0, wide, one, jnp.zeros((PATCH, BLOCK), F32), unroll=2)
    flows = correlate(False, 0, tiles_ref, sums_ref, acc_ref, soft_ref, step_ref, bend_ref, power_ref)
    for d, values in enumerate(flows):
        for strip in range(2):
            out_ref[d, pl.ds(strip, 1), :] = patch_row(values[strip * wide : (strip + 1) * wide])


def middle_flows(offsets, other, own):
    tiles = offsets.shape[1]
    return pl.pallas_call(
        flow_middle,
        out_shape=shape((2, 2, tiles), F32),
        in_specs=[spec(SMEM)] + [spec(VMEM)] * 5,
        out_specs=spec(VMEM),
        scratch_shapes=flow_scratch(tiles),
        compiler_params=params(),
        cost_estimate=pl.CostEstimate(flops=6_000_000, bytes_accessed=3_000_000, transcendentals=0),
    )(offsets, other, *own)


def flow_edges(
    offset_ref,
    rim_offset_ref,
    top_ref,
    shallow_ref,
    rim_ref,
    soft_ref,
    step_ref,
    bend_ref,
    power_ref,
    done_ref,
    out_ref,
    tiles_ref,
    sums_ref,
    acc_ref,
    next_ref,
):
    tiles = sums_ref.shape[0]
    wide = tiles // 2
    next_ref[...] = top_ref[wide].astype(F32)
    for strip in range(2):

        def one(k, carried, strip=strip):
            t = strip * wide + k
            if strip == 0:
                upper = render_rows(rim_ref[k].astype(F32), None, rim_offset_ref[0, wide + k], rim_offset_ref[1, wide + k])
            else:
                upper = render_rows(top_ref[k].astype(F32), None, offset_ref[0, k], offset_ref[1, k])
            lower = render_rows(shallow_ref[t].astype(F32), next_ref[pl.ds(t, 1), :], offset_ref[0, t], offset_ref[1, t])
            made = jnp.concatenate([upper, lower], 0)
            keep_tile(joined(made, carried), t, tiles_ref, sums_ref)
            return made

        lax.fori_loop(0, wide, one, jnp.zeros((PATCH, BLOCK), F32), unroll=2)
    flows = correlate(True, tiles, tiles_ref, sums_ref, acc_ref, soft_ref, step_ref, bend_ref, power_ref)
    for d, values in enumerate(flows):
        for strip in range(2):
            out_ref[d, pl.ds(2 * strip, 1), :] = patch_row(values[strip * wide : (strip + 1) * wide])
            out_ref[d, pl.ds(2 * strip + 1, 1), :] = done_ref[d, pl.ds(strip, 1), :]


def all_flows(offsets, rim_offsets, top, shallow, rim, own, done):
    tiles = offsets.shape[1]
    return pl.pallas_call(
        flow_edges,
        out_shape=shape((2, 4, tiles), F32),
        in_specs=[spec(SMEM)] * 2 + [spec(VMEM)] * 8,
        out_specs=spec(VMEM),
        scratch_shapes=flow_scratch(tiles),
        compiler_params=params(),
        cost_estimate=pl.CostEstimate(flops=6_000_000, bytes_accessed=3_000_000, transcendentals=0),
    )(offsets, rim_offsets, top, shallow, rim, *own, done)


def on_device(source, routes, offsets):
    strip = source[0]
    rows, cols = strip.shape
    route = routes[0]
    own_offsets = offsets[0]
    count = route.shape[0]
    devices = lax.axis_size("row")
    sections = lax.axis_size("sec")
    up = [(s, s - 1) for s in range(1, sections)]
    down = [(s, s + 1) for s in range(sections - 1)]
    below = [(r, r + 1) for r in range(devices - 1)]
    slanted = [
        (s * devices + r, (s - 1) * devices + r + 1) for s in range(1, sections) for r in range(devices - 1)
    ]

    owner = lax.div(route, jnp.int32(count))
    spot = lax.rem(route, jnp.int32(count))
    asked = owner[None, :] == jnp.arange(devices, dtype=jnp.int32)[:, None]
    lowest = jnp.min(jnp.where(asked, spot[None, :], count - 1), axis=1)
    highest = jnp.max(jnp.where(asked, spot[None, :], 0), axis=1)
    wanted = jnp.stack([lowest, highest], 1)[:, None, :]
    picked = lax.all_to_all(wanted, "row", 0, 0, tiled=True)
    blocks = blocks_of(strip)
    fellow = owner[:, None] == owner[None, :]
    lowest_here = jnp.min(jnp.where(fellow, spot[None, :], count), axis=1)
    slot = 2 * owner + (spot != lowest_here).astype(jnp.int32)

    other_offsets = lax.ppermute(own_offsets, "sec", up)
    former_offsets = lax.ppermute(own_offsets, "sec", down)
    rim_offsets = lax.ppermute(own_offsets, "row", below)
    other_rim_offsets = lax.ppermute(own_offsets, ("sec", "row"), slanted)

    out_deep = requested(picked, blocks, SPLIT, BLOCK - SPLIT)
    deep = lax.all_to_all(out_deep, "row", 0, 0, tiled=True)
    out_shallow = requested(picked, blocks, 0, SPLIT)
    shallow = lax.all_to_all(out_shallow, "row", 0, 0, tiled=True)

    middle, top_tail, bottom_tail = section_parts(slot, deep)
    former = lax.ppermute(middle, "sec", down)
    other_rim = lax.ppermute(bottom_tail, ("sec", "row"), slanted)
    other_top = lax.ppermute(top_tail, "sec", up)
    rim = lax.ppermute(bottom_tail, "row", below)
    own_shallow = shallow_part(slot, shallow)
    other_shallow = lax.ppermute(own_shallow, "sec", up)

    rim_made = render_rim(rim_offsets, rim)
    rendered, *own = render_strip(slot, own_offsets, deep, shallow, rim_made, rows, cols)
    middle_part = middle_flows(former_offsets, former, own)
    done = lax.ppermute(middle_part, "sec", up)
    flows = all_flows(other_offsets, other_rim_offsets, other_top, other_shallow, other_rim, own, done)
    return (rendered[None], flows[None])


def solution(mesh):
    placed = (P("sec", "row", None), P("sec", "row"), P("sec", None, "row"))

    return jax.shard_map(
        on_device,
        mesh=mesh,
        in_specs=placed,
        out_specs=(P("sec", "row", None), P("sec", None, "row", None)),
        check_vma=False,
    )
```

time: 265 us -> 152 us (0.57)
  the two profiles are of different devices: /device:TPU:143 before, /device:TPU:166 now
where the time goes in v1:
time: 152 us
  starting transfers between devices  64.1 us (42%)
  waiting for transfers between devices  56.7 us (37%)
  Pallas kernels  26.4 us (17%)
  local copies, waits for them, and re-layouts  1.93 us (1%)
  other arithmetic  1.53 us (1%)
    all_to_all x1, waiting for transfers between devices, on_device(): deep = lax.all_to_all(out_deep, 'row', 0, 0, tiled=True)  31.8 us
    ppermute x1, starting transfers between devices, on_device(): former_offsets = lax.ppermute(own_offsets, 'sec', down)  12.3 us
    pallas_call x1, Pallas kernels, render_strip(): pl.pallas_call(own_strip, out_shape=(shape((rows, cols), F32), tile, tile...  11.1 us
    ppermute x1, waiting for transfers between devices, on_device(): other_rim_offsets = lax.ppermute(own_offsets, ('sec', 'row'), slanted)  10.2 us
    all_to_all x1, starting transfers between devices, on_device(): shallow = lax.all_to_all(out_shallow, 'row', 0, 0, tiled=True)  10.1 us
    all_to_all x1, starting transfers between devices, on_device(): picked = lax.all_to_all(wanted, 'row', 0, 0, tiled=True)  9.18 us
    all_to_all x1, starting transfers between devices, on_device(): deep = lax.all_to_all(out_deep, 'row', 0, 0, tiled=True)  8.96 us
    all_to_all x1, waiting for transfers between devices, on_device(): shallow = lax.all_to_all(out_shallow, 'row', 0, 0, tiled=True)  6.46 us
  transfers between devices with their start and end apart: 13, of which 6 were waited for; matrix products, arithmetic and copies ran while one was open for 0% of the time, Pallas kernels for 13%

profile of v1, /device:TPU:166, one launch (start us, length us, event | category | flops | bytes accessed | tf_op | source)
XLA Modules:
  0.0 151.6 jit_solution(12589681591501280859)
XLA Ops:
  0.6 0.7 fusion
  1.3 0.7 compare_select_fusion.4
  2.0 0.2 select_reduce_fusion.1
  2.2 0.7 copy.6
  2.8 9.2 %all-to-all-start = ((s32[32,1,2]{2,1,0:T(1,128)}), s32[32,1,2]{2,1,0:T(1,128)S(1)}, u32[]{:S(2)}, u32[]{:S(2)}) async-start(s32[32,1,2]{2,1,0:T(1,128)} %copy.6), calls=%async_computation | async-start | bytes 32768 | tf_op jit(solution)/shard_map/all_to_all | solution.py:425
  12.0 0.0 copy-start.1
  12.0 1.2 copy-done.1
  13.3 0.2 shard_map.50.blocks_ref
  13.4 0.0 copy-start
  13.5 1.8 %all-to-all-done.picked_ref = s32[32,1,2]{2,1,0:T(1,128)S(1)} async-done(((s32[32,1,2]{2,1,0:T(1,128)}), s32[32,1,2]{2,1,0:T(1,128)S(1)}, u32[]{:S(2)}, u32[]{:S(2)}) %all-to-all-start) | async-done | bytes 288 | tf_op jit(solution)/shard_map/all_to_all | solution.py:425
  15.2 2.0 %shard_map.51 = bf16[64,96,128]{2,1,0:T(8,128)(2,1)} custom-call(s32[32,1,2]{2,1,0:T(1,128)S(1)} %all-to-all-done.picked_ref, bf16[32,128,128]{2,1,0:T(8,128)(2,1)S(1)} %shard_map.50.blocks_ref), custom_call_target="tpu_custom_call" | custom-call | tf_op jit(solution)/shard_map/pallas_call | solution.py:65
  17.2 0.0 copy-done
  17.3 9.0 %all-to-all-start.1 = ((bf16[64,96,128]{2,1,0:T(8,128)(2,1)}), bf16[64,96,128]{2,1,0:T(8,128)(2,1)S(1)}, u32[]{:S(2)}, u32[]{:S(2)}) async-start(bf16[64,96,128]{2,1,0:T(8,128)(2,1)} %shard_map.51), calls=%async_computation.1 | async-start | bytes 3145728 | tf_op jit(solution)/shard_map/all_to_all | solution.py:437
  26.2 0.0 copy-start.3
  26.2 2.4 %shard_map.52 = bf16[64,32,128]{2,1,0:T(8,128)(2,1)} custom-call(s32[32,1,2]{2,1,0:T(1,128)S(1)} %all-to-all-done.picked_ref, bf16[32,128,128]{2,1,0:T(8,128)(2,1)} %copy-done), custom_call_target="tpu_custom_call" | custom-call | tf_op jit(solution)/shard_map/pallas_call | solution.py:65
  28.6 0.0 copy-start.2
  28.7 31.8 %all-to-all-done.1.deep_ref = bf16[64,96,128]{2,1,0:T(8,128)(2,1)S(1)} async-done(((bf16[64,96,128]{2,1,0:T(8,128)(2,1)}), bf16[64,96,128]{2,1,0:T(8,128)(2,1)S(1)}, u32[]{:S(2)}, u32[]{:S(2)}) %all-to-all-start.1) | async-done | bytes 1572896 | tf_op jit(solution)/shard_map/all_to_all | solution.py:437
  60.4 10.1 %all-to-all-start.2 = ((bf16[64,32,128]{2,1,0:T(8,128)(2,1)}), bf16[64,32,128]{2,1,0:T(8,128)(2,1)S(1)}, u32[]{:S(2)}, u32[]{:S(2)}) async-start(bf16[64,32,128]{2,1,0:T(8,128)(2,1)} %shard_map.52), calls=%async_computation.2 | async-start | bytes 1048576 | tf_op jit(solution)/shard_map/all_to_all | solution.py:439
  70.5 0.0 copy-done.3
  70.6 0.7 shard_map.53
  71.3 6.3 %collective-permute-start.8 = (bf16[33,64,128]{2,1,0:T(8,128)(2,1)S(1)}, bf16[33,64,128]{2,1,0:T(8,128)(2,1)S(1)}, u32[]{:S(2)}, u32[]{:S(2)}) collective-permute-start(bf16[33,64,128]{2,1,0:T(8,128)(2,1)S(1)} %get-tuple-element.17), channel_id=1, source_target_pairs={{0,32},{32,64},{64,96},{96,128},{128,160},{160,192},{192,224},{224... | collective-permute-start | bytes 1622024 | tf_op jit(solution)/shard_map/ppermute | solution.py:442
  77.6 6.5 %all-to-all-done.2.shallow_ref = bf16[64,32,128]{2,1,0:T(8,128)(2,1)S(1)} async-done(((bf16[64,32,128]{2,1,0:T(8,128)(2,1)}), bf16[64,32,128]{2,1,0:T(8,128)(2,1)S(1)}, u32[]{:S(2)}, u32[]{:S(2)}) %all-to-all-start.2) | async-done | bytes 524320 | tf_op jit(solution)/shard_map/all_to_all | solution.py:439
  84.1 0.6 shard_map.56
  84.7 2.7 %collective-permute-start.5 = (bf16[32,32,128]{2,1,0:T(8,128)(2,1)S(1)}, bf16[32,32,128]{2,1,0:T(8,128)(2,1)S(1)}, u32[]{:S(2)}, u32[]{:S(2)}) collective-permute-start(bf16[32,32,128]{2,1,0:T(8,128)(2,1)S(1)} %shard_map.56), channel_id=1, source_target_pairs={{32,0},{64,32},{96,64},{128,96},{160,128},{192,160},{224,192},{256... | collective-permute-start | bytes 786440 | tf_op jit(solution)/shard_map/ppermute | solution.py:447
  87.4 2.4 %collective-permute-start.4 = (bf16[17,32,128]{2,1,0:T(8,128)(2,1)S(1)}, bf16[17,32,128]{2,1,0:T(8,128)(2,1)S(1)}, u32[]{:S(2)}, u32[]{:S(2)}) collective-permute-start(bf16[17,32,128]{2,1,0:T(8,128)(2,1)S(1)} %get-tuple-element.12), channel_id=1, source_target_pairs={{32,0},{64,32},{96,64},{128,96},{160,128},{192,160},{224,192},{256... | collective-permute-start | bytes 417800 | tf_op jit(solution)/shard_map/ppermute | solution.py:444
  89.9 1.9 %collective-permute-start.1 = (bf16[16,32,128]{2,1,0:T(8,128)(2,1)S(1)}, bf16[16,32,128]{2,1,0:T(8,128)(2,1)S(1)}, u32[]{:S(2)}, u32[]{:S(2)}) collective-permute-start(bf16[16,32,128]{2,1,0:T(8,128)(2,1)S(1)} %get-tuple-element.10), channel_id=1, source_target_pairs={{0,1},{1,2},{2,3},{3,4},{4,5},{5,6},{6,7},{7,8},{8,9},{9,10},{10,1... | collective-permute-start | bytes 393224 | tf_op jit(solution)/shard_map/ppermute | solution.py:445
  91.8 0.0 copy-done.2
  91.8 2.5 %collective-permute-start = (f32[2,32]{1,0:T(2,128)S(1)}, f32[2,32]{1,0:T(2,128)S(1)}, u32[]{:S(2)}, u32[]{:S(2)}) collective-permute-start(f32[2,32]{1,0:T(2,128)S(1)} %bitcast.25), channel_id=1, source_target_pairs={{0,1},{1,2},{2,3},{3,4},{4,5},{5,6},{6,7},{7,8},{8,9},{9,10},{10,1... | collective-permute-start | bytes 776 | tf_op jit(solution)/shard_map/ppermute | solution.py:433
  94.3 4.5 %collective-permute-done.offset_ref = f32[2,32]{1,0:T(2,128)S(1)} collective-permute-done((f32[2,32]{1,0:T(2,128)S(1)}, f32[2,32]{1,0:T(2,128)S(1)}, u32[]{:S(2)}, u32[]{:S(2)}) %collective-permute-start) | collective-permute-done | bytes 288 | tf_op jit(solution)/shard_map/ppermute | solution.py:433
  98.8 1.9 %collective-permute-start.6 = (bf16[16,32,128]{2,1,0:T(8,128)(2,1)S(1)}, bf16[16,32,128]{2,1,0:T(8,128)(2,1)S(1)}, u32[]{:S(2)}, u32[]{:S(2)}) collective-permute-start(bf16[16,32,128]{2,1,0:T(8,128)(2,1)S(1)} %get-tuple-element.10), channel_id=1, source_target_pairs={{32,1},{33,2},{34,3},{35,4},{36,5},{37,6},{38,7},{39,8},{40,9},{41... | collective-permute-start | bytes 393224 | tf_op jit(solution)/shard_map/ppermute | solution.py:443
  100.7 0.0 collective-permute-done.1.rim_ref
  100.7 12.3 %collective-permute-start.7 = (f32[2,32]{1,0:T(2,128)S(1)}, f32[2,32]{1,0:T(2,128)S(1)}, u32[]{:S(2)}, u32[]{:S(2)}) collective-permute-start(f32[2,32]{1,0:T(2,128)S(1)} %bitcast.26), channel_id=1, source_target_pairs={{0,32},{32,64},{64,96},{96,128},{128,160},{160,192},{192,224},{224... | collective-permute-start | bytes 776 | tf_op jit(solution)/shard_map/ppermute | solution.py:432
  113.0 1.2 shard_map.54.rim_ref
  114.2 11.1 %shard_map.55 = (f32[256,2048]{1,0:T(8,128)}, f32[64,64,128]{2,1,0:T(8,128)S(1)}, f32[64,64,128]{2,1,0:T(8,128)S(1)}, f32[64,64,128]{2,1,0:T(8,128)S(1)}, f32[64,128]{1,0:T(8,128)S(1)}) custom-call(s32[32]{0:T(128)S(1)} %multiply_add_fusion.slot_ref, f32[2,32]{1,0:T(2,128)S(1)} %bitcast.27, bf16[64,96,128]{2,1,0:T(8,128)(2,1)S(1)} %all-to-all-done.1.deep_ref, ...), custom_call_target="tpu_custom_call" | custom-call | flops 12000000 | bytes 3000000 | tf_op jit(solution)/shard_map/pallas_call | solution.py:249
  125.4 0.0 collective-permute-done.7.offset_ref
  125.4 1.9 %collective-permute-start.2 = (f32[2,32]{1,0:T(2,128)S(1)}, f32[2,32]{1,0:T(2,128)S(1)}, u32[]{:S(2)}, u32[]{:S(2)}) collective-permute-start(f32[2,32]{1,0:T(2,128)S(1)} %bitcast.28), channel_id=1, source_target_pairs={{32,0},{64,32},{96,64},{128,96},{160,128},{192,160},{224,192},{256... | collective-permute-start | bytes 776 | tf_op jit(solution)/shard_map/ppermute | solution.py:431
  127.3 0.0 collective-permute-done.8.other_ref
  127.3 3.7 %shard_map.57 = f32[2,2,32]{2,1,0:T(2,128)S(1)} custom-call(f32[2,32]{1,0:T(2,128)S(1)} %collective-permute-done.7.offset_ref, bf16[33,64,128]{2,1,0:T(8,128)(2,1)S(1)} %collective-permute-done.8.other_ref, f32[64,64,128]{2,1,0:T(8,128)S(1)} %get-tuple-element.13.soft_ref, f32[64,64,128]{2,1,0:T(8,128)S(1)} %get-tuple-element.14.step_ref, ...), custom_call_target="tpu_custom_call" | custom-call | flops 6000000 | bytes 3000000 | tf_op jit(solution)/shard_map/pallas_call | solution.py:339
  131.1 1.9 %collective-permute-start.9 = (f32[2,2,32]{2,1,0:T(2,128)S(1)}, f32[2,2,32]{2,1,0:T(2,128)S(1)}, u32[]{:S(2)}, u32[]{:S(2)}) collective-permute-start(f32[2,2,32]{2,1,0:T(2,128)S(1)} %shard_map.57), channel_id=1, source_target_pairs={{32,0},{64,32},{96,64},{128,96},{160,128},{192,160},{224,192},{256... | collective-permute-start | bytes 1544 | tf_op jit(solution)/shard_map/ppermute | solution.py:452
  133.0 2.1 %collective-permute-done.2.offset_ref = f32[2,32]{1,0:T(2,128)S(1)} collective-permute-done((f32[2,32]{1,0:T(2,128)S(1)}, f32[2,32]{1,0:T(2,128)S(1)}, u32[]{:S(2)}, u32[]{:S(2)}) %collective-permute-start.2) | collective-permute-done | bytes 288 | tf_op jit(solution)/shard_map/ppermute | solution.py:431
  135.1 1.9 %collective-permute-start.3 = (f32[2,32]{1,0:T(2,128)S(1)}, f32[2,32]{1,0:T(2,128)S(1)}, u32[]{:S(2)}, u32[]{:S(2)}) collective-permute-start(f32[2,32]{1,0:T(2,128)S(1)} %bitcast.29), channel_id=1, source_target_pairs={{32,1},{33,2},{34,3},{35,4},{36,5},{37,6},{38,7},{39,8},{40,9},{41... | collective-permute-start | bytes 776 | tf_op jit(solution)/shard_map/ppermute | solution.py:434
  137.0 10.2 %collective-permute-done.3.rim_offset_ref = f32[2,32]{1,0:T(2,128)S(1)} collective-permute-done((f32[2,32]{1,0:T(2,128)S(1)}, f32[2,32]{1,0:T(2,128)S(1)}, u32[]{:S(2)}, u32[]{:S(2)}) %collective-permute-start.3) | collective-permute-done | bytes 288 | tf_op jit(solution)/shard_map/ppermute | solution.py:434
  147.2 0.0 collective-permute-done.5.shallow_ref
  147.2 0.0 collective-permute-done.6.rim_ref
  147.2 0.0 collective-permute-done.4.top_ref
  147.2 0.0 collective-permute-done.9.done_ref
  147.2 4.4 %shard_map.58 = f32[2,4,32]{2,1,0:T(4,128)} custom-call(f32[2,32]{1,0:T(2,128)S(1)} %collective-permute-done.2.offset_ref, f32[2,32]{1,0:T(2,128)S(1)} %collective-permute-done.3.rim_offset_ref, bf16[17,32,128]{2,1,0:T(8,128)(2,1)S(1)} %collective-permute-done.4.top_ref, bf16[32,32,128]{2,1,0:T(8,128)(2,1)S(1)} %collective-permute-done.5.shallow_ref, ...), custom_call_target="tpu_custom_call" | custom-call | flops 6000000 | bytes 3000000 | tf_op jit(solution)/shard_map/pallas_call | solution.py:393
  (2 shorter events, 0.0 us)
Async XLA Ops:
  2.8 12.4 %all-to-all-start = ((s32[32,1,2]{2,1,0:T(1,128)}), s32[32,1,2]{2,1,0:T(1,128)S(1)}, u32[]{:S(2)}, u32[]{:S(2)}) async-start(s32[32,1,2]{2,1,0:T(1,128)} %copy.6), calls=%async_computation | async-start | bytes 32768 | tf_op jit(solution)/shard_map/all_to_all | solution.py:425
  12.0 1.2 copy-start.1
  13.4 3.8 %copy-start = (bf16[32,128,128]{2,1,0:T(8,128)(2,1)}, bf16[32,128,128]{2,1,0:T(8,128)(2,1)S(1)}, u32[]{:S(2)}) copy-start(bf16[32,128,128]{2,1,0:T(8,128)(2,1)S(1)} %shard_map.50.blocks_ref) | copy-start | bytes 3145732
  17.3 43.2 %all-to-all-start.1 = ((bf16[64,96,128]{2,1,0:T(8,128)(2,1)}), bf16[64,96,128]{2,1,0:T(8,128)(2,1)S(1)}, u32[]{:S(2)}, u32[]{:S(2)}) async-start(bf16[64,96,128]{2,1,0:T(8,128)(2,1)} %shard_map.51), calls=%async_computation.1 | async-start | bytes 3145728 | tf_op jit(solution)/shard_map/all_to_all | solution.py:437
  26.2 44.3 %copy-start.3 = (s32[1,32]{1,0:T(1,128)S(1)}, s32[1,32]{1,0:T(1,128)}, u32[]{:S(2)}) copy-start(s32[1,32]{1,0:T(1,128)} %param.4) | copy-start | bytes 388
  28.6 63.2 %copy-start.2 = (f32[1,2,32]{2,1,0:T(2,128)S(1)}, f32[1,2,32]{2,1,0:T(2,128)}, u32[]{:S(2)}) copy-start(f32[1,2,32]{2,1,0:T(2,128)} %param.5) | copy-start | bytes 772
  60.4 23.7 %all-to-all-start.2 = ((bf16[64,32,128]{2,1,0:T(8,128)(2,1)}), bf16[64,32,128]{2,1,0:T(8,128)(2,1)S(1)}, u32[]{:S(2)}, u32[]{:S(2)}) async-start(bf16[64,32,128]{2,1,0:T(8,128)(2,1)} %shard_map.52), calls=%async_computation.2 | async-start | bytes 1048576 | tf_op jit(solution)/shard_map/all_to_all | solution.py:439
  71.3 56.0 %collective-permute-start.8 = (bf16[33,64,128]{2,1,0:T(8,128)(2,1)S(1)}, bf16[33,64,128]{2,1,0:T(8,128)(2,1)S(1)}, u32[]{:S(2)}, u32[]{:S(2)}) collective-permute-start(bf16[33,64,128]{2,1,0:T(8,128)(2,1)S(1)} %get-tuple-element.17), channel_id=1, source_target_pairs={{0,32},{32,64},{64,96},{96,128},{128,160},{160,192},{192,224},{224... | collective-permute-start | bytes 1622024 | tf_op jit(solution)/shard_map/ppermute | solution.py:442
  84.7 62.5 %collective-permute-start.5 = (bf16[32,32,128]{2,1,0:T(8,128)(2,1)S(1)}, bf16[32,32,128]{2,1,0:T(8,128)(2,1)S(1)}, u32[]{:S(2)}, u32[]{:S(2)}) collective-permute-start(bf16[32,32,128]{2,1,0:T(8,128)(2,1)S(1)} %shard_map.56), channel_id=1, source_target_pairs={{32,0},{64,32},{96,64},{128,96},{160,128},{192,160},{224,192},{256... | collective-permute-start | bytes 786440 | tf_op jit(solution)/shard_map/ppermute | solution.py:447
  87.4 59.8 %collective-permute-start.4 = (bf16[17,32,128]{2,1,0:T(8,128)(2,1)S(1)}, bf16[17,32,128]{2,1,0:T(8,128)(2,1)S(1)}, u32[]{:S(2)}, u32[]{:S(2)}) collective-permute-start(bf16[17,32,128]{2,1,0:T(8,128)(2,1)S(1)} %get-tuple-element.12), channel_id=1, source_target_pairs={{32,0},{64,32},{96,64},{128,96},{160,128},{192,160},{224,192},{256... | collective-permute-start | bytes 417800 | tf_op jit(solution)/shard_map/ppermute | solution.py:444
  89.9 10.9 %collective-permute-start.1 = (bf16[16,32,128]{2,1,0:T(8,128)(2,1)S(1)}, bf16[16,32,128]{2,1,0:T(8,128)(2,1)S(1)}, u32[]{:S(2)}, u32[]{:S(2)}) collective-permute-start(bf16[16,32,128]{2,1,0:T(8,128)(2,1)S(1)} %get-tuple-element.10), channel_id=1, source_target_pairs={{0,1},{1,2},{2,3},{3,4},{4,5},{5,6},{6,7},{7,8},{8,9},{9,10},{10,1... | collective-permute-start | bytes 393224 | tf_op jit(solution)/shard_map/ppermute | solution.py:445
  91.8 7.0 %collective-permute-start = (f32[2,32]{1,0:T(2,128)S(1)}, f32[2,32]{1,0:T(2,128)S(1)}, u32[]{:S(2)}, u32[]{:S(2)}) collective-permute-start(f32[2,32]{1,0:T(2,128)S(1)} %bitcast.25), channel_id=1, source_target_pairs={{0,1},{1,2},{2,3},{3,4},{4,5},{5,6},{6,7},{7,8},{8,9},{9,10},{10,1... | collective-permute-start | bytes 776 | tf_op jit(solution)/shard_map/ppermute | solution.py:433
  98.8 48.4 %collective-permute-start.6 = (bf16[16,32,128]{2,1,0:T(8,128)(2,1)S(1)}, bf16[16,32,128]{2,1,0:T(8,128)(2,1)S(1)}, u32[]{:S(2)}, u32[]{:S(2)}) collective-permute-start(bf16[16,32,128]{2,1,0:T(8,128)(2,1)S(1)} %get-tuple-element.10), channel_id=1, source_target_pairs={{32,1},{33,2},{34,3},{35,4},{36,5},{37,6},{38,7},{39,8},{40,9},{41... | collective-permute-start | bytes 393224 | tf_op jit(solution)/shard_map/ppermute | solution.py:443
  100.7 24.7 %collective-permute-start.7 = (f32[2,32]{1,0:T(2,128)S(1)}, f32[2,32]{1,0:T(2,128)S(1)}, u32[]{:S(2)}, u32[]{:S(2)}) collective-permute-start(f32[2,32]{1,0:T(2,128)S(1)} %bitcast.26), channel_id=1, source_target_pairs={{0,32},{32,64},{64,96},{96,128},{128,160},{160,192},{192,224},{224... | collective-permute-start | bytes 776 | tf_op jit(solution)/shard_map/ppermute | solution.py:432
  125.4 9.7 %collective-permute-start.2 = (f32[2,32]{1,0:T(2,128)S(1)}, f32[2,32]{1,0:T(2,128)S(1)}, u32[]{:S(2)}, u32[]{:S(2)}) collective-permute-start(f32[2,32]{1,0:T(2,128)S(1)} %bitcast.28), channel_id=1, source_target_pairs={{32,0},{64,32},{96,64},{128,96},{160,128},{192,160},{224,192},{256... | collective-permute-start | bytes 776 | tf_op jit(solution)/shard_map/ppermute | solution.py:431
  131.1 16.1 %collective-permute-start.9 = (f32[2,2,32]{2,1,0:T(2,128)S(1)}, f32[2,2,32]{2,1,0:T(2,128)S(1)}, u32[]{:S(2)}, u32[]{:S(2)}) collective-permute-start(f32[2,2,32]{2,1,0:T(2,128)S(1)} %shard_map.57), channel_id=1, source_target_pairs={{32,0},{64,32},{96,64},{128,96},{160,128},{192,160},{224,192},{256... | collective-permute-start | bytes 1544 | tf_op jit(solution)/shard_map/ppermute | solution.py:452
  135.1 12.1 %collective-permute-start.3 = (f32[2,32]{1,0:T(2,128)S(1)}, f32[2,32]{1,0:T(2,128)S(1)}, u32[]{:S(2)}, u32[]{:S(2)}) collective-permute-start(f32[2,32]{1,0:T(2,128)S(1)} %bitcast.29), channel_id=1, source_target_pairs={{32,1},{33,2},{34,3},{35,4},{36,5},{37,6},{38,7},{39,8},{40,9},{41... | collective-permute-start | bytes 776 | tf_op jit(solution)/shard_map/ppermute | solution.py:434

commit v2 on v1

v2 whole, which is shorter than its diff:
```python
import functools

import jax
import jax.numpy as jnp
from jax import lax
from jax.experimental import pallas as pl
from jax.experimental.pallas import tpu as pltpu
from jax.sharding import PartitionSpec as P


peak_floor = 64.0
tiny_value = 1e-06
BLOCK = 128
PATCH = 64
SPLIT = 32
VMEM = pltpu.VMEM
SMEM = pltpu.SMEM
F32 = jnp.float32
BF16 = jnp.bfloat16


def spec(space):
    return pl.BlockSpec(memory_space=space)


def shape(dims, dtype):
    return jax.ShapeDtypeStruct(dims, dtype)


def params(limit=14 << 20):
    return pltpu.CompilerParams(vmem_limit_bytes=limit)


def ask_blocks(route_ref, out_ref, slot_ref):
    devices = out_ref.shape[0]
    count = route_ref.shape[1]
    route = jnp.broadcast_to(route_ref[...], (devices, count))
    owner = lax.div(route, jnp.int32(count))
    spot = lax.rem(route, jnp.int32(count))
    asked = owner == lax.broadcasted_iota(jnp.int32, route.shape, 0)
    lowest = jnp.min(jnp.where(asked, spot, count - 1), axis=1, keepdims=True)
    highest = jnp.max(jnp.where(asked, spot, 0), axis=1, keepdims=True)
    lowest_here = jnp.sum(jnp.where(asked, lowest, 0), axis=0, keepdims=True)
    slot_ref[...] = 2 * owner[:1] + (spot[:1] != lowest_here).astype(jnp.int32)
    lane = lax.broadcasted_iota(jnp.int32, (devices, 2), 1)
    both = jnp.where(lane == 0, lowest, highest)
    for o in range(devices):
        out_ref[o] = both[o : o + 1]


def wanted_blocks(routes, devices):
    return pl.pallas_call(
        ask_blocks,
        out_shape=(shape((devices, 1, 2), jnp.int32), shape(routes.shape, jnp.int32)),
        in_specs=[spec(VMEM)],
        out_specs=(spec(VMEM), spec(VMEM)),
        compiler_params=params(),
    )(routes)


def cut_blocks(strip_ref, out_ref):
    wide = strip_ref.shape[1] // BLOCK
    for i in range(strip_ref.shape[0] // BLOCK):
        for k in range(wide):
            out_ref[i * wide + k] = strip_ref[i * BLOCK : (i + 1) * BLOCK, k * BLOCK : (k + 1) * BLOCK]


def blocks_of(strip):
    rows, cols = strip.shape
    return pl.pallas_call(
        cut_blocks,
        out_shape=shape((rows // BLOCK * (cols // BLOCK), BLOCK, BLOCK), strip.dtype),
        in_specs=[spec(VMEM)],
        out_specs=spec(VMEM),
        compiler_params=params(),
        cost_estimate=pl.CostEstimate(flops=0, bytes_accessed=2_000_000, transcendentals=0),
    )(strip)


def pack_requested(row_from, rows, picked_ref, blocks_ref, out_ref, sem):
    def one(i, carry):
        spot = picked_ref[i // 2, 0, i % 2]
        pltpu.make_async_copy(blocks_ref.at[spot, pl.ds(row_from, rows), :], out_ref.at[i], sem).start()
        return carry

    lax.fori_loop(0, out_ref.shape[0], one, 0, unroll=8)
    pltpu.make_async_copy(out_ref, out_ref, sem).wait()


def requested(picked, blocks, row_from, rows):
    slots = 2 * picked.shape[0]
    return pl.pallas_call(
        functools.partial(pack_requested, row_from, rows),
        out_shape=shape((slots, rows, BLOCK), blocks.dtype),
        in_specs=[spec(SMEM), spec(VMEM)],
        out_specs=spec(pl.ANY),
        scratch_shapes=[pltpu.SemaphoreType.DMA],
        compiler_params=params(55_000_000),
    )(picked, blocks)


def pack_middle(slot_ref, deep_ref, out_ref, next_ref):
    count = next_ref.shape[0]

    def one(b, carry):
        s = slot_ref[b]
        out_ref[b] = deep_ref[s, pl.ds(0, 64), :]
        next_ref[pl.ds(b, 1), :] = deep_ref[s, pl.ds(64, 16), :].astype(F32)[0:1]
        return carry

    lax.fori_loop(0, count, one, 0, unroll=8)
    out_ref[count, pl.ds(0, count), :] = next_ref[...].astype(BF16)
    out_ref[count, pl.ds(count, PATCH - count), :] = jnp.zeros((PATCH - count, BLOCK), BF16)


def middle_rows(slot, deep):
    count = slot.shape[0]
    return pl.pallas_call(
        pack_middle,
        out_shape=shape((count + 1, PATCH, BLOCK), BF16),
        in_specs=[spec(SMEM), spec(VMEM)],
        out_specs=spec(VMEM),
        scratch_shapes=[VMEM((count, BLOCK), F32)],
        compiler_params=params(),
    )(slot, deep)


def pack_tails(slot_ref, deep_ref, top_ref, bottom_ref, first_ref):
    half = bottom_ref.shape[0]

    def tails(b, carry):
        top = slot_ref[b]
        bottom = slot_ref[half + b]
        top_ref[b] = deep_ref[top, pl.ds(64, 32), :]
        bottom_ref[b] = deep_ref[bottom, pl.ds(64, 32), :]
        first_ref[pl.ds(b, 1), :] = deep_ref[top, pl.ds(0, 16), :].astype(F32)[0:1]
        first_ref[pl.ds(half + b, 1), :] = deep_ref[bottom, pl.ds(0, 16), :].astype(F32)[0:1]
        return carry

    lax.fori_loop(0, half, tails, 0, unroll=4)
    top_ref[half] = first_ref[...].astype(BF16)


def tail_rows(slot, deep):
    count = slot.shape[0]
    half = count // 2
    return pl.pallas_call(
        pack_tails,
        out_shape=(shape((half + 1, 32, BLOCK), BF16), shape((half, 32, BLOCK), BF16)),
        in_specs=[spec(SMEM), spec(VMEM)],
        out_specs=(spec(VMEM), spec(VMEM)),
        scratch_shapes=[VMEM((count, BLOCK), F32)],
        compiler_params=params(),
    )(slot, deep)


def pack_shallow(slot_ref, shallow_ref, out_ref):
    def one(b, carry):
        out_ref[b] = shallow_ref[slot_ref[b]]
        return carry

    lax.fori_loop(0, out_ref.shape[0], one, 0, unroll=4)


def shallow_part(slot, shallow):
    return pl.pallas_call(
        pack_shallow,
        out_shape=shape((slot.shape[0], *shallow.shape[1:]), BF16),
        in_specs=[spec(SMEM), spec(VMEM)],
        out_specs=spec(VMEM),
        compiler_params=params(),
    )(slot, shallow)


def mixed_across(square, across):
    lane = lax.broadcasted_iota(jnp.int32, square.shape, 1)
    moved = jnp.where(lane == BLOCK - 1, square, pltpu.roll(square, BLOCK - 1, 1))
    return (1.0 - across) * square + across * moved


def render_rows(square, following, downward, across):
    rows = square.shape[0]
    mixed = mixed_across(square, across)
    below = mixed if following is None else mixed_across(following, across)
    row = lax.broadcasted_iota(jnp.int32, square.shape, 0)
    moved = jnp.where(row == rows - 1, below, pltpu.roll(mixed, rows - 1, 0))
    return (1.0 - downward) * mixed + downward * moved


def joined(made, carried):
    lane = lax.broadcasted_iota(jnp.int32, made.shape, 1)
    return jnp.where(lane < BLOCK - PATCH // 2, made, carried)


def same_patch():
    half = PATCH // 2
    one = lax.broadcasted_iota(jnp.int32, (BLOCK, BLOCK), 0)
    two = lax.broadcasted_iota(jnp.int32, (BLOCK, BLOCK), 1)
    return ((((one + half) // PATCH) % 2) == (((two + half) // PATCH) % 2)).astype(F32)


def per_patch(values):
    return jnp.dot(values, same_patch(), precision=lax.Precision.HIGHEST)


def row_filters():
    half = PATCH // 2
    source = lax.broadcasted_iota(jnp.int32, (BLOCK, BLOCK), 0)
    target = lax.broadcasted_iota(jnp.int32, (BLOCK, BLOCK), 1)
    place = target % PATCH
    after = jnp.where(place == half - 1, target + 1 - PATCH, target + 1) % BLOCK
    before = jnp.where(place == half, target - 1 + PATCH, target - 1) % BLOCK
    after = (source == after).astype(F32)
    before = (source == before).astype(F32)
    itself = (source == target).astype(F32)
    pair = after + before
    twice = itself + itself
    return jnp.concatenate([0.25 * (twice + pair), after - before, twice - pair], 1).astype(BF16)


def folded(values):
    return jnp.sum(values.reshape(-1, 8, BLOCK), axis=0)


def write_filters(out_ref):
    filters = row_filters()
    out_ref[pl.ds(0, BLOCK), :] = filters
    out_ref[pl.ds(BLOCK, BLOCK), :] = filters


def filter_matrix():
    return pl.pallas_call(
        write_filters,
        out_shape=shape((2 * BLOCK, 3 * BLOCK), BF16),
        out_specs=spec(VMEM),
        compiler_params=params(),
    )()


def filter_tile(b, filter_ref, t, soft_ref, step_ref, bend_ref, parts_ref):
    high = b.astype(BF16)
    rest = (b - high.astype(F32)).astype(BF16)
    made = jnp.dot(jnp.concatenate([high, rest], 1), filter_ref[...], preferred_element_type=F32)
    soft_ref[t] = made[:, :BLOCK]
    step_ref[t] = made[:, BLOCK : 2 * BLOCK]
    bend_ref[t] = made[:, 2 * BLOCK :]
    parts_ref[t] = folded(b * b)


def own_strip(
    slot_ref, offset_ref, deep_ref, shallow_ref, filter_ref, image_ref, first_ref, soft_ref, step_ref, bend_ref, power_ref, mixed_ref, tall_ref, parts_ref, sums_ref, sem
):
    wide = first_ref.shape[0]
    half = PATCH // 2
    rows = 2 * BLOCK

    def across(b, carry):
        s = slot_ref[b]
        square = jnp.concatenate([shallow_ref[s], deep_ref[s]], 0)
        mixed = mixed_across(square.astype(F32), offset_ref[1, b])
        mixed_ref[b, pl.ds(0, BLOCK), :] = mixed
        mixed_ref[b, pl.ds(BLOCK, 1), :] = mixed[BLOCK - 1 :]
        return carry

    lax.fori_loop(0, 2 * wide, across, 0, unroll=8)
    tall_ref[0] = jnp.zeros((rows, BLOCK), F32)

    def down(k, carry):
        for strip in range(2):
            b = strip * wide + k
            y = offset_ref[0, b]
            made = (1.0 - y) * mixed_ref[b, pl.ds(0, BLOCK), :] + y * mixed_ref[b, pl.ds(1, BLOCK), :]
            tall_ref[k + 1, pl.ds(strip * BLOCK, BLOCK), :] = made
            if strip == 0:
                first_ref[k] = made[:half]
        pltpu.make_async_copy(
            tall_ref.at[k + 1], image_ref.at[:, pl.ds(pl.multiple_of(k * BLOCK, BLOCK), BLOCK)], sem
        ).start()
        return carry

    lax.fori_loop(0, wide, down, 0, unroll=4)
    groups = (1, 3, 2)

    def tile(k, g):
        rows_of = pl.ds(g * PATCH - half, PATCH)
        return joined(tall_ref[k + 1, rows_of, :], tall_ref[k, rows_of, :])

    def add_up(k, carry):
        for i, g in enumerate(groups):
            parts_ref[i * wide + k] = folded(tile(k, g))
        return carry

    lax.fori_loop(0, wide, add_up, 0, unroll=4)
    sums_ref[...] = per_patch(jnp.sum(parts_ref[...], axis=1)) / float(PATCH * PATCH)

    def filtered(k, carry):
        for i, g in enumerate(groups):
            t = i * wide + k
            filter_tile(tile(k, g) - sums_ref[pl.ds(t, 1), :], filter_ref, t, soft_ref, step_ref, bend_ref, parts_ref)
        return carry

    lax.fori_loop(0, wide, filtered, 0, unroll=4)
    power_ref[...] = per_patch(jnp.sum(parts_ref[...], axis=1))
    pltpu.make_async_copy(image_ref, image_ref, sem).wait()


def tile_outs(tiles):
    tile = shape((tiles, PATCH, BLOCK), F32)
    return (tile, tile, tile, shape((tiles, BLOCK), F32))


def render_strip(slot, offsets, deep, shallow, filters, rows, cols):
    blocks = slot.shape[0]
    wide = cols // BLOCK
    tiles = 3 * wide
    return pl.pallas_call(
        own_strip,
        out_shape=(shape((rows, cols), F32), shape((wide, PATCH // 2, BLOCK), F32), *tile_outs(tiles)),
        in_specs=[spec(SMEM)] * 2 + [spec(VMEM)] * 3,
        out_specs=(spec(pl.ANY),) + (spec(VMEM),) * 5,
        scratch_shapes=[
            VMEM((blocks, BLOCK + 8, BLOCK), F32),
            VMEM((wide + 1, rows, BLOCK), F32),
            VMEM((tiles, 8, BLOCK), F32),
            VMEM((tiles, BLOCK), F32),
            pltpu.SemaphoreType.DMA,
        ],
        compiler_params=params(),
        cost_estimate=pl.CostEstimate(flops=12_000_000, bytes_accessed=3_000_000, transcendentals=0),
    )(slot, offsets, deep, shallow, filters)


def own_zero(offset_ref, rim_ref, first_ref, filter_ref, soft_ref, step_ref, bend_ref, power_ref, tall_ref, parts_ref, sums_ref):
    wide = rim_ref.shape[0]

    def one(k, carried):
        made = render_rows(rim_ref[k].astype(F32), None, offset_ref[0, wide + k], offset_ref[1, wide + k])
        whole = jnp.concatenate([made, first_ref[k]], 0)
        tile = joined(whole, carried)
        tall_ref[k] = tile
        parts_ref[k] = folded(tile)
        return whole

    lax.fori_loop(0, wide, one, jnp.zeros((PATCH, BLOCK), F32), unroll=4)
    sums_ref[...] = per_patch(jnp.sum(parts_ref[...], axis=1)) / float(PATCH * PATCH)

    def filtered(k, carry):
        filter_tile(tall_ref[k] - sums_ref[pl.ds(k, 1), :], filter_ref, k, soft_ref, step_ref, bend_ref, parts_ref)
        return carry

    lax.fori_loop(0, wide, filtered, 0, unroll=8)
    power_ref[...] = per_patch(jnp.sum(parts_ref[...], axis=1))


def rim_tiles(offsets, rim, first, filters):
    wide = rim.shape[0]
    return pl.pallas_call(
        own_zero,
        out_shape=tile_outs(wide),
        in_specs=[spec(SMEM)] + [spec(VMEM)] * 3,
        out_specs=(spec(VMEM),) * 4,
        scratch_shapes=[VMEM((wide, PATCH, BLOCK), F32), VMEM((wide, 8, BLOCK), F32), VMEM((wide, BLOCK), F32)],
        compiler_params=params(),
        cost_estimate=pl.CostEstimate(flops=3_000_000, bytes_accessed=1_000_000, transcendentals=0),
    )(offsets, rim, first, filters)


PAD = 8


def keep_tile(tile, t, tiles_ref, sums_ref):
    tiles_ref[t, pl.ds(PAD, PATCH), :] = tile
    tiles_ref[t, pl.ds(PAD - 1, 1), :] = tile[PATCH - 1 :]
    tiles_ref[t, pl.ds(PAD + PATCH, 1), :] = tile[:1]
    sums_ref[pl.ds(t, 1), :] = jnp.sum(tile, axis=0, keepdims=True)


def correlate(own_is_first, own, tiles_ref, sums_ref, acc_ref):
    area = float(PATCH * PATCH)
    tiles = sums_ref.shape[0]
    wide = tiles // 2
    sums_ref[...] = per_patch(sums_ref[...]) / area
    for strip, (refs, base) in enumerate(own):
        soft_ref, step_ref, bend_ref, _ = refs

        def one(k, carry, strip=strip, base=base, soft_ref=soft_ref, step_ref=step_ref, bend_ref=bend_ref):
            t = strip * wide + k
            mean = sums_ref[pl.ds(t, 1), :]
            o = tiles_ref[t, pl.ds(PAD, PATCH), :]
            after = tiles_ref[t, pl.ds(PAD + 1, PATCH), :]
            before = tiles_ref[t, pl.ds(PAD - 1, PATCH), :]
            pair = after + before
            twice = o + o
            soft = 0.25 * (twice + pair) - mean
            step = after - before
            bend = twice - pair
            flat = o - mean
            own_soft = soft_ref[base + k]
            products = (flat * flat, own_soft * step, own_soft * bend, step_ref[base + k] * soft, bend_ref[base + k] * soft)
            for q, product in enumerate(products):
                acc_ref[pl.ds(q * tiles + t, 1), :] = jnp.sum(product, axis=0, keepdims=True)
            return carry

        lax.fori_loop(0, wide, one, 0, unroll=2)
    totals = per_patch(acc_ref[...])
    part = [totals[q * tiles : (q + 1) * tiles] for q in range(5)]
    power = jnp.concatenate([refs[3][pl.ds(base, wide), :] for refs, base in own], 0)
    scale = 1.0 / (jnp.sqrt(part[0] / area + tiny_value) * jnp.sqrt(power / area + tiny_value))
    signs = (1.0, -1.0) if own_is_first else (-1.0, 1.0)
    down = signs[0] * part[1] * scale / (2.0 * jnp.maximum(part[2] * scale, peak_floor))
    across = signs[1] * part[3] * scale / (2.0 * jnp.maximum(part[4] * scale, peak_floor))
    return down, across


def patch_row(values):
    lane = lax.broadcasted_iota(jnp.int32, values.shape, 1)
    row = lax.broadcasted_iota(jnp.int32, values.shape, 0)
    chosen = jnp.where(lane % 2 == 0, values, pltpu.roll(values, PATCH, 1))
    return jnp.sum(jnp.where(lane // 2 == row, chosen, 0.0), axis=0, keepdims=True)[:, : 2 * values.shape[0]]


def flow_scratch(tiles):
    return [
        VMEM((tiles, PATCH + 2 * PAD, BLOCK), F32),
        VMEM((tiles, BLOCK), F32),
        VMEM((5 * tiles, BLOCK), F32),
        VMEM((tiles, BLOCK), F32),
    ]


def flow_middle(offset_ref, other_ref, soft_ref, step_ref, bend_ref, power_ref, out_ref, tiles_ref, sums_ref, acc_ref, next_ref):
    tiles = sums_ref.shape[0]
    wide = tiles // 2
    next_ref[...] = other_ref[tiles, pl.ds(0, tiles), :].astype(F32)
    for strip in range(2):

        def one(k, carried, strip=strip):
            t = strip * wide + k
            made = render_rows(other_ref[t].astype(F32), next_ref[pl.ds(t, 1), :], offset_ref[0, t], offset_ref[1, t])
            keep_tile(joined(made, carried), t, tiles_ref, sums_ref)
            return made

        lax.fori_loop(0, wide, one, jnp.zeros((PATCH, BLOCK), F32), unroll=8)
    refs = (soft_ref, step_ref, bend_ref, power_ref)
    flows = correlate(False, ((refs, 0), (refs, wide)), tiles_ref, sums_ref, acc_ref)
    for d, values in enumerate(flows):
        for strip in range(2):
            out_ref[d, pl.ds(strip, 1), :] = patch_row(values[strip * wide : (strip + 1) * wide])


def middle_flows(offsets, other, own):
    tiles = offsets.shape[1]
    return pl.pallas_call(
        flow_middle,
        out_shape=shape((2, 2, tiles), F32),
        in_specs=[spec(SMEM)] + [spec(VMEM)] * 5,
        out_specs=spec(VMEM),
        scratch_shapes=flow_scratch(tiles),
        compiler_params=params(),
        cost_estimate=pl.CostEstimate(flops=6_000_000, bytes_accessed=3_000_000, transcendentals=0),
    )(offsets, other, *own)


def flow_edges(
    offset_ref,
    rim_offset_ref,
    top_ref,
    shallow_ref,
    rim_ref,
    *refs,
):
    zero_refs, own_refs, (out_ref, tiles_ref, sums_ref, acc_ref, next_ref) = refs[:4], refs[4:8], refs[8:]
    tiles = sums_ref.shape[0]
    wide = tiles // 2
    next_ref[...] = top_ref[wide].astype(F32)
    for strip in range(2):

        def one(k, carried, strip=strip):
            t = strip * wide + k
            if strip == 0:
                upper = render_rows(rim_ref[k].astype(F32), None, rim_offset_ref[0, wide + k], rim_offset_ref[1, wide + k])
            else:
                upper = render_rows(top_ref[k].astype(F32), None, offset_ref[0, k], offset_ref[1, k])
            lower = render_rows(shallow_ref[t].astype(F32), next_ref[pl.ds(t, 1), :], offset_ref[0, t], offset_ref[1, t])
            made = jnp.concatenate([upper, lower], 0)
            keep_tile(joined(made, carried), t, tiles_ref, sums_ref)
            return made

        lax.fori_loop(0, wide, one, jnp.zeros((PATCH, BLOCK), F32), unroll=8)
    flows = correlate(True, ((zero_refs, 0), (own_refs, tiles)), tiles_ref, sums_ref, acc_ref)
    for d, values in enumerate(flows):
        for strip in range(2):
            out_ref[d, pl.ds(strip, 1), :] = patch_row(values[strip * wide : (strip + 1) * wide])


def edge_flows(offsets, rim_offsets, top, shallow, rim, zero, own):
    tiles = offsets.shape[1]
    return pl.pallas_call(
        flow_edges,
        out_shape=shape((2, 2, tiles), F32),
        in_specs=[spec(SMEM)] * 2 + [spec(VMEM)] * 11,
        out_specs=spec(VMEM),
        scratch_shapes=flow_scratch(tiles),
        compiler_params=params(),
        cost_estimate=pl.CostEstimate(flops=6_000_000, bytes_accessed=3_000_000, transcendentals=0),
    )(offsets, rim_offsets, top, shallow, rim, *zero, *own)


def merge_rows(edge_ref, middle_ref, out_ref):
    for d in range(2):
        for i in range(2):
            out_ref[d, pl.ds(2 * i, 1), :] = edge_ref[d, pl.ds(i, 1), :]
            out_ref[d, pl.ds(2 * i + 1, 1), :] = middle_ref[d, pl.ds(i, 1), :]


def merge_flows(edge, middle):
    return pl.pallas_call(
        merge_rows,
        out_shape=shape((2, 4, edge.shape[2]), F32),
        in_specs=[spec(VMEM)] * 2,
        out_specs=spec(VMEM),
        compiler_params=params(),
    )(edge, middle)


def on_device(source, routes, offsets):
    strip = source[0]
    rows, cols = strip.shape
    own_offsets = offsets[0]
    count = routes.shape[1]
    devices = lax.axis_size("row")
    sections = lax.axis_size("sec")
    up = [(s, s - 1) for s in range(1, sections)]
    down = [(s, s + 1) for s in range(sections - 1)]
    below = [(r, r + 1) for r in range(devices - 1)]
    slanted = [
        (s * devices + r, (s - 1) * devices + r + 1) for s in range(1, sections) for r in range(devices - 1)
    ]

    wanted, slot = wanted_blocks(routes, devices)
    slot = slot.reshape(count)
    picked = lax.all_to_all(wanted, "row", 0, 0, tiled=True)
    blocks = blocks_of(strip)

    other_offsets = lax.ppermute(own_offsets, "sec", up)
    former_offsets = lax.ppermute(own_offsets, "sec", down)
    rim_offsets = lax.ppermute(own_offsets, "row", below)
    other_rim_offsets = lax.ppermute(own_offsets, ("sec", "row"), slanted)

    out_deep = requested(picked, blocks, SPLIT, BLOCK - SPLIT)
    deep = lax.all_to_all(out_deep, "row", 0, 0, tiled=True)
    out_shallow = requested(picked, blocks, 0, SPLIT)
    shallow = lax.all_to_all(out_shallow, "row", 0, 0, tiled=True)

    middle = middle_rows(slot, deep)
    former = lax.ppermute(middle, "sec", down)
    top_tail, bottom_tail = tail_rows(slot, deep)
    rim = lax.ppermute(bottom_tail, "row", below)
    other_rim = lax.ppermute(bottom_tail, ("sec", "row"), slanted)
    other_top = lax.ppermute(top_tail, "sec", up)
    filters = filter_matrix()
    own_shallow = shallow_part(slot, shallow)
    other_shallow = lax.ppermute(own_shallow, "sec", up)

    rendered, first, *own = render_strip(slot, own_offsets, deep, shallow, filters, rows, cols)
    zero = rim_tiles(rim_offsets, rim, first, filters)
    middle_part = middle_flows(former_offsets, former, own)
    done = lax.ppermute(middle_part, "sec", up)
    edge_part = edge_flows(other_offsets, other_rim_offsets, other_top, other_shallow, other_rim, zero, own)
    flows = merge_flows(edge_part, done)
    return (rendered[None], flows[None])


def solution(mesh):
    placed = (P("sec", "row", None), P("sec", "row"), P("sec", None, "row"))

    return jax.shard_map(
        on_device,
        mesh=mesh,
        in_specs=placed,
        out_specs=(P("sec", "row", None), P("sec", None, "row", None)),
        check_vma=False,
    )
```

time: 152 us -> 140 us (0.921)
  the two profiles are of different devices: /device:TPU:166 before, /device:TPU:134 now
where the time goes in v2:
time: 140 us; the launch traced here: 139 us
  waiting for transfers between devices  65.2 us (47%)
  starting transfers between devices  52.1 us (37%)
  Pallas kernels  19.3 us (14%)
  local copies, waits for them, and re-layouts  1.88 us (1%)
    all_to_all x1, waiting for transfers between devices, on_device(): deep = lax.all_to_all(out_deep, 'row', 0, 0, tiled=True)  38 us
    all_to_all x1, waiting for transfers between devices, on_device(): shallow = lax.all_to_all(out_shallow, 'row', 0, 0, tiled=True)  11 us
    ppermute x1, starting transfers between devices, on_device(): former_offsets = lax.ppermute(own_offsets, 'sec', down)  10.6 us
    all_to_all x1, starting transfers between devices, on_device(): picked = lax.all_to_all(wanted, 'row', 0, 0, tiled=True)  9.3 us
    all_to_all x1, waiting for transfers between devices, on_device(): picked = lax.all_to_all(wanted, 'row', 0, 0, tiled=True)  6.76 us
    ppermute x1, starting transfers between devices, on_device(): former = lax.ppermute(middle, 'sec', down)  6.32 us
    ppermute x1, waiting for transfers between devices, on_device(): done = lax.ppermute(middle_part, 'sec', up)  4.92 us
    pallas_call x2, Pallas kernels, requested(): pl.pallas_call(functools.partial(pack_requested, row_from, rows), out_sha...  4.43 us
  transfers between devices with their start and end apart: 13, of which 6 were waited for; matrix products, arithmetic and copies ran while one was open for 0% of the time, Pallas kernels for 11%

profile of v2, /device:TPU:134, one launch (start us, length us, event | category | flops | bytes accessed | tf_op | source)
XLA Modules:
  0.0 139.4 jit_solution(5965518639671111963)
XLA Ops:
  0.6 0.0 copy-start.3
  0.6 0.6 copy-done.3
  1.3 0.8 shard_map.50
  2.1 9.3 %all-to-all-start = ((s32[32,1,2]{2,1,0:T(1,128)}), s32[32,1,2]{2,1,0:T(1,128)S(1)}, u32[]{:S(2)}, u32[]{:S(2)}) async-start(s32[32,1,2]{2,1,0:T(1,128)} %get-tuple-element.17), calls=%async_computation | async-start | bytes 32768 | tf_op jit(solution)/shard_map/all_to_all | solution.py:542
  11.4 0.0 copy-start.1
  11.4 1.2 copy-done.1
  12.6 0.2 shard_map.51.blocks_ref
  12.8 0.0 copy-start
  12.8 6.8 %all-to-all-done.picked_ref = s32[32,1,2]{2,1,0:T(1,128)S(1)} async-done(((s32[32,1,2]{2,1,0:T(1,128)}), s32[32,1,2]{2,1,0:T(1,128)S(1)}, u32[]{:S(2)}, u32[]{:S(2)}) %all-to-all-start) | async-done | bytes 288 | tf_op jit(solution)/shard_map/all_to_all | solution.py:542
  19.6 2.0 %shard_map.52 = bf16[64,96,128]{2,1,0:T(8,128)(2,1)} custom-call(s32[32,1,2]{2,1,0:T(1,128)S(1)} %all-to-all-done.picked_ref, bf16[32,128,128]{2,1,0:T(8,128)(2,1)S(1)} %shard_map.51.blocks_ref), custom_call_target="tpu_custom_call" | custom-call | tf_op jit(solution)/shard_map/pallas_call | solution.py:92
  21.6 0.0 copy-done
  21.6 4.0 %all-to-all-start.1 = ((bf16[64,96,128]{2,1,0:T(8,128)(2,1)}), bf16[64,96,128]{2,1,0:T(8,128)(2,1)S(1)}, u32[]{:S(2)}, u32[]{:S(2)}) async-start(bf16[64,96,128]{2,1,0:T(8,128)(2,1)} %shard_map.52), calls=%async_computation.1 | async-start | bytes 3145728 | tf_op jit(solution)/shard_map/all_to_all | solution.py:551
  25.6 2.4 %shard_map.53 = bf16[64,32,128]{2,1,0:T(8,128)(2,1)} custom-call(s32[32,1,2]{2,1,0:T(1,128)S(1)} %all-to-all-done.picked_ref, bf16[32,128,128]{2,1,0:T(8,128)(2,1)} %copy-done), custom_call_target="tpu_custom_call" | custom-call | tf_op jit(solution)/shard_map/pallas_call | solution.py:92
  28.0 38.0 %all-to-all-done.1.deep_ref = bf16[64,96,128]{2,1,0:T(8,128)(2,1)S(1)} async-done(((bf16[64,96,128]{2,1,0:T(8,128)(2,1)}), bf16[64,96,128]{2,1,0:T(8,128)(2,1)S(1)}, u32[]{:S(2)}, u32[]{:S(2)}) %all-to-all-start.1) | async-done | bytes 1572896 | tf_op jit(solution)/shard_map/all_to_all | solution.py:551
  66.0 3.9 %all-to-all-start.2 = ((bf16[64,32,128]{2,1,0:T(8,128)(2,1)}), bf16[64,32,128]{2,1,0:T(8,128)(2,1)S(1)}, u32[]{:S(2)}, u32[]{:S(2)}) async-start(bf16[64,32,128]{2,1,0:T(8,128)(2,1)} %shard_map.53), calls=%async_computation.2 | async-start | bytes 1048576 | tf_op jit(solution)/shard_map/all_to_all | solution.py:553
  69.9 0.6 shard_map.60
  70.5 0.0 copy-start.2
  70.5 6.3 %collective-permute-start.8 = (bf16[33,64,128]{2,1,0:T(8,128)(2,1)S(1)}, bf16[33,64,128]{2,1,0:T(8,128)(2,1)S(1)}, u32[]{:S(2)}, u32[]{:S(2)}) collective-permute-start(bf16[33,64,128]{2,1,0:T(8,128)(2,1)S(1)} %shard_map.60), channel_id=1, source_target_pairs={{0,32},{32,64},{64,96},{96,128},{128,160},{160,192},{192,224},{224... | collective-permute-start | bytes 1622024 | tf_op jit(solution)/shard_map/ppermute | solution.py:556
  76.9 11.0 %all-to-all-done.2.shallow_ref = bf16[64,32,128]{2,1,0:T(8,128)(2,1)S(1)} async-done(((bf16[64,32,128]{2,1,0:T(8,128)(2,1)}), bf16[64,32,128]{2,1,0:T(8,128)(2,1)S(1)}, u32[]{:S(2)}, u32[]{:S(2)}) %all-to-all-start.2) | async-done | bytes 524320 | tf_op jit(solution)/shard_map/all_to_all | solution.py:553
  87.9 0.6 shard_map.57
  88.5 2.7 %collective-permute-start.3 = (bf16[32,32,128]{2,1,0:T(8,128)(2,1)S(1)}, bf16[32,32,128]{2,1,0:T(8,128)(2,1)S(1)}, u32[]{:S(2)}, u32[]{:S(2)}) collective-permute-start(bf16[32,32,128]{2,1,0:T(8,128)(2,1)S(1)} %shard_map.57), channel_id=1, source_target_pairs={{32,0},{64,32},{96,64},{128,96},{160,128},{192,160},{224,192},{256... | collective-permute-start | bytes 786440 | tf_op jit(solution)/shard_map/ppermute | solution.py:563
  91.3 0.6 shard_map.56
  91.9 2.4 %collective-permute-start.2 = (bf16[17,32,128]{2,1,0:T(8,128)(2,1)S(1)}, bf16[17,32,128]{2,1,0:T(8,128)(2,1)S(1)}, u32[]{:S(2)}, u32[]{:S(2)}) collective-permute-start(bf16[17,32,128]{2,1,0:T(8,128)(2,1)S(1)} %get-tuple-element.19), channel_id=1, source_target_pairs={{32,0},{64,32},{96,64},{128,96},{160,128},{192,160},{224,192},{256... | collective-permute-start | bytes 417800 | tf_op jit(solution)/shard_map/ppermute | solution.py:560
  94.3 1.3 collective-permute-start.6
  95.6 0.0 copy-done.2
  95.6 4.1 %collective-permute-start.5 = (f32[2,32]{1,0:T(2,128)S(1)}, f32[2,32]{1,0:T(2,128)S(1)}, u32[]{:S(2)}, u32[]{:S(2)}) collective-permute-start(f32[2,32]{1,0:T(2,128)S(1)} %bitcast.10), channel_id=1, source_target_pairs={{0,1},{1,2},{2,3},{3,4},{4,5},{5,6},{6,7},{7,8},{8,9},{9,10},{10,1... | collective-permute-start | bytes 776 | tf_op jit(solution)/shard_map/ppermute | solution.py:547
  99.7 0.8 collective-permute-done.5.offset_ref
  100.5 2.4 %collective-permute-start.4 = (bf16[16,32,128]{2,1,0:T(8,128)(2,1)S(1)}, bf16[16,32,128]{2,1,0:T(8,128)(2,1)S(1)}, u32[]{:S(2)}, u32[]{:S(2)}) collective-permute-start(bf16[16,32,128]{2,1,0:T(8,128)(2,1)S(1)} %get-tuple-element.20), channel_id=1, source_target_pairs={{32,1},{33,2},{34,3},{35,4},{36,5},{37,6},{38,7},{39,8},{40,9},{41... | collective-permute-start | bytes 393224 | tf_op jit(solution)/shard_map/ppermute | solution.py:559
  103.0 3.9 %shard_map.55 = (f32[256,2048]{1,0:T(8,128)}, f32[16,32,128]{2,1,0:T(8,128)S(1)}, f32[48,64,128]{2,1,0:T(8,128)S(1)}, f32[48,64,128]{2,1,0:T(8,128)S(1)}, f32[48...) custom-call(s32[32]{0:T(128)S(1)} %bitcast.9, f32[2,32]{1,0:T(2,128)S(1)} %bitcast.11, ...), custom_call_target="tpu_custom_call" | custom-call | flops 12000000 | bytes 3000000 | tf_op jit(solution)/shard_map/pallas_call | solution.py:316
  106.9 0.0 collective-permute-done.6.rim_ref
  106.9 10.6 %collective-permute-start.7 = (f32[2,32]{1,0:T(2,128)S(1)}, f32[2,32]{1,0:T(2,128)S(1)}, u32[]{:S(2)}, u32[]{:S(2)}) collective-permute-start(f32[2,32]{1,0:T(2,128)S(1)} %bitcast.12), channel_id=1, source_target_pairs={{0,32},{32,64},{64,96},{96,128},{128,160},{160,192},{192,224},{224... | collective-permute-start | bytes 776 | tf_op jit(solution)/shard_map/ppermute | solution.py:546
  117.4 2.0 %shard_map.58 = (f32[16,64,128]{2,1,0:T(8,128)S(1)}, f32[16,64,128]{2,1,0:T(8,128)S(1)}, f32[16,64,128]{2,1,0:T(8,128)S(1)}, f32[16,128]{1,0:T(8,128)S(1)}) custom-call(f32[2,32]{1,0:T(2,128)S(1)} %collective-permute-done.5.offset_ref, bf16[16,32,128]{2,1,0:T(8,128)(2,1)S(1)} %collective-permute-done.6.rim_ref, ...), custom_call_target="tpu_custom_call" | custom-call | flops 3000000 | bytes 1000000 | tf_op jit(solution)/shard_map/pallas_call | solution.py:357
  119.5 0.0 collective-permute-done.7.offset_ref
  119.5 1.9 %collective-permute-start = (f32[2,32]{1,0:T(2,128)S(1)}, f32[2,32]{1,0:T(2,128)S(1)}, u32[]{:S(2)}, u32[]{:S(2)}) collective-permute-start(f32[2,32]{1,0:T(2,128)S(1)} %bitcast.13), channel_id=1, source_target_pairs={{32,0},{64,32},{96,64},{128,96},{160,128},{192,160},{224,192},{256... | collective-permute-start | bytes 776 | tf_op jit(solution)/shard_map/ppermute | solution.py:545
  121.4 0.0 collective-permute-done.8.other_ref
  121.4 1.3 collective-permute-start.1
  122.7 2.8 %shard_map.61 = f32[2,2,32]{2,1,0:T(2,128)S(1)} custom-call(f32[2,32]{1,0:T(2,128)S(1)} %collective-permute-done.7.offset_ref, bf16[33,64,128]{2,1,0:T(8,128)(2,1)S(1)} %collective-permute-done.8.other_ref, f32[48,64,128]{2,1,0:T(8,128)S(1)} %get-tuple-element.26.refs_4_.soft_ref, f32[48,64,128]{2,1,0:T(8,128)S(1)} %get-tuple-element.27.refs_5_.step_ref, ...), custom_call_target="tpu_custom_call" | custom-call | flops 6000000 | bytes 3000000 | tf_op jit(solution)/shard_map/pallas_call | solution.py:453
  125.5 3.7 %collective-permute-done.offset_ref = f32[2,32]{1,0:T(2,128)S(1)} collective-permute-done((f32[2,32]{1,0:T(2,128)S(1)}, f32[2,32]{1,0:T(2,128)S(1)}, u32[]{:S(2)}, u32[]{:S(2)}) %collective-permute-start) | collective-permute-done | bytes 288 | tf_op jit(solution)/shard_map/ppermute | solution.py:545
  129.2 1.9 %collective-permute-start.9 = (f32[2,2,32]{2,1,0:T(2,128)S(1)}, f32[2,2,32]{2,1,0:T(2,128)S(1)}, u32[]{:S(2)}, u32[]{:S(2)}) collective-permute-start(f32[2,2,32]{2,1,0:T(2,128)S(1)} %shard_map.61), channel_id=1, source_target_pairs={{32,0},{64,32},{96,64},{128,96},{160,128},{192,160},{224,192},{256... | collective-permute-start | bytes 1544 | tf_op jit(solution)/shard_map/ppermute | solution.py:568
  131.1 0.0 collective-permute-done.1.rim_offset_ref
  131.1 0.0 collective-permute-done.3.shallow_ref
  131.1 0.0 collective-permute-done.4.rim_ref
  131.1 0.0 collective-permute-done.2.top_ref
  131.1 2.8 %shard_map.59.edge_ref = f32[2,2,32]{2,1,0:T(2,128)S(1)} custom-call(f32[2,32]{1,0:T(2,128)S(1)} %collective-permute-done.offset_ref, f32[2,32]{1,0:T(2,128)S(1)} %collective-permute-done.1.rim_offset_ref, bf16[17,32,128]{2,1,0:T(8,128)(2,1)S(1)} %collective-permute-done.2.top_ref, bf16[32,32,128]{2,1,0:T(8,128)(2,1)S(1)} %collective-permute-done.3.shallow_ref, ...), custom_call_target="tpu_custom_call" | custom-call | flops 6000000 | bytes 3000000 | tf_op jit(solution)/shard_map/pallas_call | solution.py:498
  133.9 4.9 %collective-permute-done.9.middle_ref = f32[2,2,32]{2,1,0:T(2,128)S(1)} collective-permute-done((f32[2,2,32]{2,1,0:T(2,128)S(1)}, f32[2,2,32]{2,1,0:T(2,128)S(1)}, u32[]{:S(2)}, u32[]{:S(2)}) %collective-permute-start.9) | collective-permute-done | bytes 544 | tf_op jit(solution)/shard_map/ppermute | solution.py:568
  138.8 0.6 shard_map.62
  (1 shorter events, 0.0 us)
Async XLA Ops:
  0.6 0.7 copy-start.3
  2.1 17.5 %all-to-all-start = ((s32[32,1,2]{2,1,0:T(1,128)}), s32[32,1,2]{2,1,0:T(1,128)S(1)}, u32[]{:S(2)}, u32[]{:S(2)}) async-start(s32[32,1,2]{2,1,0:T(1,128)} %get-tuple-element.17), calls=%async_computation | async-start | bytes 32768 | tf_op jit(solution)/shard_map/all_to_all | solution.py:542
  11.4 1.2 copy-start.1
  12.8 8.8 %copy-start = (bf16[32,128,128]{2,1,0:T(8,128)(2,1)}, bf16[32,128,128]{2,1,0:T(8,128)(2,1)S(1)}, u32[]{:S(2)}) copy-start(bf16[32,128,128]{2,1,0:T(8,128)(2,1)S(1)} %shard_map.51.blocks_ref) | copy-start | bytes 3145732
  21.6 44.4 %all-to-all-start.1 = ((bf16[64,96,128]{2,1,0:T(8,128)(2,1)}), bf16[64,96,128]{2,1,0:T(8,128)(2,1)S(1)}, u32[]{:S(2)}, u32[]{:S(2)}) async-start(bf16[64,96,128]{2,1,0:T(8,128)(2,1)} %shard_map.52), calls=%async_computation.1 | async-start | bytes 3145728 | tf_op jit(solution)/shard_map/all_to_all | solution.py:551
  66.0 21.9 %all-to-all-start.2 = ((bf16[64,32,128]{2,1,0:T(8,128)(2,1)}), bf16[64,32,128]{2,1,0:T(8,128)(2,1)S(1)}, u32[]{:S(2)}, u32[]{:S(2)}) async-start(bf16[64,32,128]{2,1,0:T(8,128)(2,1)} %shard_map.53), calls=%async_computation.2 | async-start | bytes 1048576 | tf_op jit(solution)/shard_map/all_to_all | solution.py:553
  70.5 25.1 %copy-start.2 = (f32[1,2,32]{2,1,0:T(2,128)S(1)}, f32[1,2,32]{2,1,0:T(2,128)}, u32[]{:S(2)}) copy-start(f32[1,2,32]{2,1,0:T(2,128)} %param.5) | copy-start | bytes 772
  70.5 50.9 %collective-permute-start.8 = (bf16[33,64,128]{2,1,0:T(8,128)(2,1)S(1)}, bf16[33,64,128]{2,1,0:T(8,128)(2,1)S(1)}, u32[]{:S(2)}, u32[]{:S(2)}) collective-permute-start(bf16[33,64,128]{2,1,0:T(8,128)(2,1)S(1)} %shard_map.60), channel_id=1, source_target_pairs={{0,32},{32,64},{64,96},{96,128},{128,160},{160,192},{192,224},{224... | collective-permute-start | bytes 1622024 | tf_op jit(solution)/shard_map/ppermute | solution.py:556
  88.5 42.6 %collective-permute-start.3 = (bf16[32,32,128]{2,1,0:T(8,128)(2,1)S(1)}, bf16[32,32,128]{2,1,0:T(8,128)(2,1)S(1)}, u32[]{:S(2)}, u32[]{:S(2)}) collective-permute-start(bf16[32,32,128]{2,1,0:T(8,128)(2,1)S(1)} %shard_map.57), channel_id=1, source_target_pairs={{32,0},{64,32},{96,64},{128,96},{160,128},{192,160},{224,192},{256... | collective-permute-start | bytes 786440 | tf_op jit(solution)/shard_map/ppermute | solution.py:563
  91.9 39.2 %collective-permute-start.2 = (bf16[17,32,128]{2,1,0:T(8,128)(2,1)S(1)}, bf16[17,32,128]{2,1,0:T(8,128)(2,1)S(1)}, u32[]{:S(2)}, u32[]{:S(2)}) collective-permute-start(bf16[17,32,128]{2,1,0:T(8,128)(2,1)S(1)} %get-tuple-element.19), channel_id=1, source_target_pairs={{32,0},{64,32},{96,64},{128,96},{160,128},{192,160},{224,192},{256... | collective-permute-start | bytes 417800 | tf_op jit(solution)/shard_map/ppermute | solution.py:560
  94.3 12.6 %collective-permute-start.6 = (bf16[16,32,128]{2,1,0:T(8,128)(2,1)S(1)}, bf16[16,32,128]{2,1,0:T(8,128)(2,1)S(1)}, u32[]{:S(2)}, u32[]{:S(2)}) collective-permute-start(bf16[16,32,128]{2,1,0:T(8,128)(2,1)S(1)} %get-tuple-element.20), channel_id=1, source_target_pairs={{0,1},{1,2},{2,3},{3,4},{4,5},{5,6},{6,7},{7,8},{8,9},{9,10},{10,1... | collective-permute-start | bytes 393224 | tf_op jit(solution)/shard_map/ppermute | solution.py:558
  95.6 4.9 %collective-permute-start.5 = (f32[2,32]{1,0:T(2,128)S(1)}, f32[2,32]{1,0:T(2,128)S(1)}, u32[]{:S(2)}, u32[]{:S(2)}) collective-permute-start(f32[2,32]{1,0:T(2,128)S(1)} %bitcast.10), channel_id=1, source_target_pairs={{0,1},{1,2},{2,3},{3,4},{4,5},{5,6},{6,7},{7,8},{8,9},{9,10},{10,1... | collective-permute-start | bytes 776 | tf_op jit(solution)/shard_map/ppermute | solution.py:547
  100.5 30.6 %collective-permute-start.4 = (bf16[16,32,128]{2,1,0:T(8,128)(2,1)S(1)}, bf16[16,32,128]{2,1,0:T(8,128)(2,1)S(1)}, u32[]{:S(2)}, u32[]{:S(2)}) collective-permute-start(bf16[16,32,128]{2,1,0:T(8,128)(2,1)S(1)} %get-tuple-element.20), channel_id=1, source_target_pairs={{32,1},{33,2},{34,3},{35,4},{36,5},{37,6},{38,7},{39,8},{40,9},{41... | collective-permute-start | bytes 393224 | tf_op jit(solution)/shard_map/ppermute | solution.py:559
  106.9 12.6 %collective-permute-start.7 = (f32[2,32]{1,0:T(2,128)S(1)}, f32[2,32]{1,0:T(2,128)S(1)}, u32[]{:S(2)}, u32[]{:S(2)}) collective-permute-start(f32[2,32]{1,0:T(2,128)S(1)} %bitcast.12), channel_id=1, source_target_pairs={{0,32},{32,64},{64,96},{96,128},{128,160},{160,192},{192,224},{224... | collective-permute-start | bytes 776 | tf_op jit(solution)/shard_map/ppermute | solution.py:546
  119.5 9.7 %collective-permute-start = (f32[2,32]{1,0:T(2,128)S(1)}, f32[2,32]{1,0:T(2,128)S(1)}, u32[]{:S(2)}, u32[]{:S(2)}) collective-permute-start(f32[2,32]{1,0:T(2,128)S(1)} %bitcast.13), channel_id=1, source_target_pairs={{32,0},{64,32},{96,64},{128,96},{160,128},{192,160},{224,192},{256... | collective-permute-start | bytes 776 | tf_op jit(solution)/shard_map/ppermute | solution.py:545
  121.4 9.7 %collective-permute-start.1 = (f32[2,32]{1,0:T(2,128)S(1)}, f32[2,32]{1,0:T(2,128)S(1)}, u32[]{:S(2)}, u32[]{:S(2)}) collective-permute-start(f32[2,32]{1,0:T(2,128)S(1)} %bitcast.14), channel_id=1, source_target_pairs={{32,1},{33,2},{34,3},{35,4},{36,5},{37,6},{38,7},{39,8},{40,9},{41... | collective-permute-start | bytes 776 | tf_op jit(solution)/shard_map/ppermute | solution.py:548
  129.2 9.7 %collective-permute-start.9 = (f32[2,2,32]{2,1,0:T(2,128)S(1)}, f32[2,2,32]{2,1,0:T(2,128)S(1)}, u32[]{:S(2)}, u32[]{:S(2)}) collective-permute-start(f32[2,2,32]{2,1,0:T(2,128)S(1)} %shard_map.61), channel_id=1, source_target_pairs={{32,0},{64,32},{96,64},{128,96},{160,128},{192,160},{224,192},{256... | collective-permute-start | bytes 1544 | tf_op jit(solution)/shard_map/ppermute | solution.py:568

commit v3 on v2

--- a/solution.py
+++ b/solution.py
@@ -83,7 +83,7 @@
         pltpu.make_async_copy(blocks_ref.at[spot, pl.ds(row_from, rows), :], out_ref.at[i], sem).start()
         return carry
 
-    lax.fori_loop(0, out_ref.shape[0], one, 0, unroll=8)
+    lax.fori_loop(0, out_ref.shape[0], one, 0, unroll=64)
     pltpu.make_async_copy(out_ref, out_ref, sem).wait()
 
 
@@ -401,7 +401,7 @@
                 acc_ref[pl.ds(q * tiles + t, 1), :] = jnp.sum(product, axis=0, keepdims=True)
             return carry
 
-        lax.fori_loop(0, wide, one, 0, unroll=2)
+        lax.fori_loop(0, wide, one, 0, unroll=4)
     totals = per_patch(acc_ref[...])
     part = [totals[q * tiles : (q + 1) * tiles] for q in range(5)]
     power = jnp.concatenate([refs[3][pl.ds(base, wide), :] for refs, base in own], 0)
@@ -440,7 +440,7 @@
             keep_tile(joined(made, carried), t, tiles_ref, sums_ref)
             return made
 
-        lax.fori_loop(0, wide, one, jnp.zeros((PATCH, BLOCK), F32), unroll=8)
+        lax.fori_loop(0, wide, one, jnp.zeros((PATCH, BLOCK), F32), unroll=16)
     refs = (soft_ref, step_ref, bend_ref, power_ref)
     flows = correlate(False, ((refs, 0), (refs, wide)), tiles_ref, sums_ref, acc_ref)
     for d, values in enumerate(flows):
@@ -486,7 +486,7 @@
             keep_tile(joined(made, carried), t, tiles_ref, sums_ref)
             return made
 
-        lax.fori_loop(0, wide, one, jnp.zeros((PATCH, BLOCK), F32), unroll=8)
+        lax.fori_loop(0, wide, one, jnp.zeros((PATCH, BLOCK), F32), unroll=16)
     flows = correlate(True, ((zero_refs, 0), (own_refs, tiles)), tiles_ref, sums_ref, acc_ref)
     for d, values in enumerate(flows):
         for strip in range(2):

time: 140 us -> 140 us (level)
  no operation moved by 1% of the time
where the time goes in v3:
time: 140 us; the launch traced here: 139 us
  waiting for transfers between devices  66 us (47%)
  starting transfers between devices  52.1 us (37%)
  Pallas kernels  18.5 us (13%)
  local copies, waits for them, and re-layouts  1.88 us (1%)
    all_to_all x1, waiting for transfers between devices, on_device(): deep = lax.all_to_all(out_deep, 'row', 0, 0, tiled=True)  38.4 us
    all_to_all x1, waiting for transfers between devices, on_device(): shallow = lax.all_to_all(out_shallow, 'row', 0, 0, tiled=True)  11 us
    ppermute x1, starting transfers between devices, on_device(): former_offsets = lax.ppermute(own_offsets, 'sec', down)  10.6 us
    all_to_all x1, starting transfers between devices, on_device(): picked = lax.all_to_all(wanted, 'row', 0, 0, tiled=True)  9.3 us
    all_to_all x1, waiting for transfers between devices, on_device(): picked = lax.all_to_all(wanted, 'row', 0, 0, tiled=True)  6.76 us
    ppermute x1, starting transfers between devices, on_device(): former = lax.ppermute(middle, 'sec', down)  6.32 us
    ppermute x1, waiting for transfers between devices, on_device(): done = lax.ppermute(middle_part, 'sec', up)  5.13 us
    ppermute x1, starting transfers between devices, on_device(): rim_offsets = lax.ppermute(own_offsets, 'row', below)  4.08 us
  transfers between devices with their start and end apart: 13, of which 6 were waited for; matrix products, arithmetic and copies ran while one was open for 0% of the time, Pallas kernels for 11%

profile of v3, /device:TPU:134, one launch (start us, length us, event | category | flops | bytes accessed | tf_op | source)
XLA Modules:
  0.0 139.4 jit_solution(7295396643179026857)
XLA Ops:
  0.6 0.0 copy-start.3
  0.6 0.6 copy-done.3
  1.3 0.8 shard_map.50
  2.1 9.3 %all-to-all-start = ((s32[32,1,2]{2,1,0:T(1,128)}), s32[32,1,2]{2,1,0:T(1,128)S(1)}, u32[]{:S(2)}, u32[]{:S(2)}) async-start(s32[32,1,2]{2,1,0:T(1,128)} %get-tuple-element.17), calls=%async_computation | async-start | bytes 32768 | tf_op jit(solution)/shard_map/all_to_all | solution.py:542
  11.4 0.0 copy-start.1
  11.4 1.2 copy-done.1
  12.6 0.2 shard_map.51.blocks_ref
  12.8 0.0 copy-start
  12.8 6.8 %all-to-all-done.picked_ref = s32[32,1,2]{2,1,0:T(1,128)S(1)} async-done(((s32[32,1,2]{2,1,0:T(1,128)}), s32[32,1,2]{2,1,0:T(1,128)S(1)}, u32[]{:S(2)}, u32[]{:S(2)}) %all-to-all-start) | async-done | bytes 288 | tf_op jit(solution)/shard_map/all_to_all | solution.py:542
  19.6 1.9 %shard_map.52 = bf16[64,96,128]{2,1,0:T(8,128)(2,1)} custom-call(s32[32,1,2]{2,1,0:T(1,128)S(1)} %all-to-all-done.picked_ref, bf16[32,128,128]{2,1,0:T(8,128)(2,1)S(1)} %shard_map.51.blocks_ref), custom_call_target="tpu_custom_call" | custom-call | tf_op jit(solution)/shard_map/pallas_call | solution.py:92
  21.5 0.0 copy-done
  21.5 4.0 %all-to-all-start.1 = ((bf16[64,96,128]{2,1,0:T(8,128)(2,1)}), bf16[64,96,128]{2,1,0:T(8,128)(2,1)S(1)}, u32[]{:S(2)}, u32[]{:S(2)}) async-start(bf16[64,96,128]{2,1,0:T(8,128)(2,1)} %shard_map.52), calls=%async_computation.1 | async-start | bytes 3145728 | tf_op jit(solution)/shard_map/all_to_all | solution.py:551
  25.5 2.1 %shard_map.53 = bf16[64,32,128]{2,1,0:T(8,128)(2,1)} custom-call(s32[32,1,2]{2,1,0:T(1,128)S(1)} %all-to-all-done.picked_ref, bf16[32,128,128]{2,1,0:T(8,128)(2,1)} %copy-done), custom_call_target="tpu_custom_call" | custom-call | tf_op jit(solution)/shard_map/pallas_call | solution.py:92
  27.6 38.4 %all-to-all-done.1.deep_ref = bf16[64,96,128]{2,1,0:T(8,128)(2,1)S(1)} async-done(((bf16[64,96,128]{2,1,0:T(8,128)(2,1)}), bf16[64,96,128]{2,1,0:T(8,128)(2,1)S(1)}, u32[]{:S(2)}, u32[]{:S(2)}) %all-to-all-start.1) | async-done | bytes 1572896 | tf_op jit(solution)/shard_map/all_to_all | solution.py:551
  65.9 3.9 %all-to-all-start.2 = ((bf16[64,32,128]{2,1,0:T(8,128)(2,1)}), bf16[64,32,128]{2,1,0:T(8,128)(2,1)S(1)}, u32[]{:S(2)}, u32[]{:S(2)}) async-start(bf16[64,32,128]{2,1,0:T(8,128)(2,1)} %shard_map.53), calls=%async_computation.2 | async-start | bytes 1048576 | tf_op jit(solution)/shard_map/all_to_all | solution.py:553
  69.8 0.6 shard_map.60
  70.4 0.0 copy-start.2
  70.5 6.3 %collective-permute-start.8 = (bf16[33,64,128]{2,1,0:T(8,128)(2,1)S(1)}, bf16[33,64,128]{2,1,0:T(8,128)(2,1)S(1)}, u32[]{:S(2)}, u32[]{:S(2)}) collective-permute-start(bf16[33,64,128]{2,1,0:T(8,128)(2,1)S(1)} %shard_map.60), channel_id=1, source_target_pairs={{0,32},{32,64},{64,96},{96,128},{128,160},{160,192},{192,224},{224... | collective-permute-start | bytes 1622024 | tf_op jit(solution)/shard_map/ppermute | solution.py:556
  76.8 11.0 %all-to-all-done.2.shallow_ref = bf16[64,32,128]{2,1,0:T(8,128)(2,1)S(1)} async-done(((bf16[64,32,128]{2,1,0:T(8,128)(2,1)}), bf16[64,32,128]{2,1,0:T(8,128)(2,1)S(1)}, u32[]{:S(2)}, u32[]{:S(2)}) %all-to-all-start.2) | async-done | bytes 524320 | tf_op jit(solution)/shard_map/all_to_all | solution.py:553
  87.8 0.6 shard_map.57
  88.4 2.7 %collective-permute-start.3 = (bf16[32,32,128]{2,1,0:T(8,128)(2,1)S(1)}, bf16[32,32,128]{2,1,0:T(8,128)(2,1)S(1)}, u32[]{:S(2)}, u32[]{:S(2)}) collective-permute-start(bf16[32,32,128]{2,1,0:T(8,128)(2,1)S(1)} %shard_map.57), channel_id=1, source_target_pairs={{32,0},{64,32},{96,64},{128,96},{160,128},{192,160},{224,192},{256... | collective-permute-start | bytes 786440 | tf_op jit(solution)/shard_map/ppermute | solution.py:563
  91.2 0.6 shard_map.56
  91.8 2.4 %collective-permute-start.2 = (bf16[17,32,128]{2,1,0:T(8,128)(2,1)S(1)}, bf16[17,32,128]{2,1,0:T(8,128)(2,1)S(1)}, u32[]{:S(2)}, u32[]{:S(2)}) collective-permute-start(bf16[17,32,128]{2,1,0:T(8,128)(2,1)S(1)} %get-tuple-element.19), channel_id=1, source_target_pairs={{32,0},{64,32},{96,64},{128,96},{160,128},{192,160},{224,192},{256... | collective-permute-start | bytes 417800 | tf_op jit(solution)/shard_map/ppermute | solution.py:560
  94.2 1.3 collective-permute-start.6
  95.5 0.0 copy-done.2
  95.5 4.1 %collective-permute-start.5 = (f32[2,32]{1,0:T(2,128)S(1)}, f32[2,32]{1,0:T(2,128)S(1)}, u32[]{:S(2)}, u32[]{:S(2)}) collective-permute-start(f32[2,32]{1,0:T(2,128)S(1)} %bitcast.10), channel_id=1, source_target_pairs={{0,1},{1,2},{2,3},{3,4},{4,5},{5,6},{6,7},{7,8},{8,9},{9,10},{10,1... | collective-permute-start | bytes 776 | tf_op jit(solution)/shard_map/ppermute | solution.py:547
  99.6 0.8 collective-permute-done.5.offset_ref
  100.4 2.4 %collective-permute-start.4 = (bf16[16,32,128]{2,1,0:T(8,128)(2,1)S(1)}, bf16[16,32,128]{2,1,0:T(8,128)(2,1)S(1)}, u32[]{:S(2)}, u32[]{:S(2)}) collective-permute-start(bf16[16,32,128]{2,1,0:T(8,128)(2,1)S(1)} %get-tuple-element.20), channel_id=1, source_target_pairs={{32,1},{33,2},{34,3},{35,4},{36,5},{37,6},{38,7},{39,8},{40,9},{41... | collective-permute-start | bytes 393224 | tf_op jit(solution)/shard_map/ppermute | solution.py:559
  102.9 3.9 %shard_map.55 = (f32[256,2048]{1,0:T(8,128)}, f32[16,32,128]{2,1,0:T(8,128)S(1)}, f32[48,64,128]{2,1,0:T(8,128)S(1)}, f32[48,64,128]{2,1,0:T(8,128)S(1)}, f32[48...) custom-call(s32[32]{0:T(128)S(1)} %bitcast.9, f32[2,32]{1,0:T(2,128)S(1)} %bitcast.11, ...), custom_call_target="tpu_custom_call" | custom-call | flops 12000000 | bytes 3000000 | tf_op jit(solution)/shard_map/pallas_call | solution.py:316
  106.8 0.0 collective-permute-done.6.rim_ref
  106.8 10.6 %collective-permute-start.7 = (f32[2,32]{1,0:T(2,128)S(1)}, f32[2,32]{1,0:T(2,128)S(1)}, u32[]{:S(2)}, u32[]{:S(2)}) collective-permute-start(f32[2,32]{1,0:T(2,128)S(1)} %bitcast.12), channel_id=1, source_target_pairs={{0,32},{32,64},{64,96},{96,128},{128,160},{160,192},{192,224},{224... | collective-permute-start | bytes 776 | tf_op jit(solution)/shard_map/ppermute | solution.py:546
  117.4 2.0 %shard_map.58 = (f32[16,64,128]{2,1,0:T(8,128)S(1)}, f32[16,64,128]{2,1,0:T(8,128)S(1)}, f32[16,64,128]{2,1,0:T(8,128)S(1)}, f32[16,128]{1,0:T(8,128)S(1)}) custom-call(f32[2,32]{1,0:T(2,128)S(1)} %collective-permute-done.5.offset_ref, bf16[16,32,128]{2,1,0:T(8,128)(2,1)S(1)} %collective-permute-done.6.rim_ref, ...), custom_call_target="tpu_custom_call" | custom-call | flops 3000000 | bytes 1000000 | tf_op jit(solution)/shard_map/pallas_call | solution.py:357
  119.4 0.0 collective-permute-done.7.offset_ref
  119.4 1.9 %collective-permute-start = (f32[2,32]{1,0:T(2,128)S(1)}, f32[2,32]{1,0:T(2,128)S(1)}, u32[]{:S(2)}, u32[]{:S(2)}) collective-permute-start(f32[2,32]{1,0:T(2,128)S(1)} %bitcast.13), channel_id=1, source_target_pairs={{32,0},{64,32},{96,64},{128,96},{160,128},{192,160},{224,192},{256... | collective-permute-start | bytes 776 | tf_op jit(solution)/shard_map/ppermute | solution.py:545
  121.3 0.0 collective-permute-done.8.other_ref
  121.3 1.3 collective-permute-start.1
  122.6 2.5 %shard_map.61 = f32[2,2,32]{2,1,0:T(2,128)S(1)} custom-call(f32[2,32]{1,0:T(2,128)S(1)} %collective-permute-done.7.offset_ref, bf16[33,64,128]{2,1,0:T(8,128)(2,1)S(1)} %collective-permute-done.8.other_ref, f32[48,64,128]{2,1,0:T(8,128)S(1)} %get-tuple-element.26.refs_4_.soft_ref, f32[48,64,128]{2,1,0:T(8,128)S(1)} %get-tuple-element.27.refs_5_.step_ref, ...), custom_call_target="tpu_custom_call" | custom-call | flops 6000000 | bytes 3000000 | tf_op jit(solution)/shard_map/pallas_call | solution.py:453
  125.2 3.9 %collective-permute-done.offset_ref = f32[2,32]{1,0:T(2,128)S(1)} collective-permute-done((f32[2,32]{1,0:T(2,128)S(1)}, f32[2,32]{1,0:T(2,128)S(1)}, u32[]{:S(2)}, u32[]{:S(2)}) %collective-permute-start) | collective-permute-done | bytes 288 | tf_op jit(solution)/shard_map/ppermute | solution.py:545
  129.1 1.9 %collective-permute-start.9 = (f32[2,2,32]{2,1,0:T(2,128)S(1)}, f32[2,2,32]{2,1,0:T(2,128)S(1)}, u32[]{:S(2)}, u32[]{:S(2)}) collective-permute-start(f32[2,2,32]{2,1,0:T(2,128)S(1)} %shard_map.61), channel_id=1, source_target_pairs={{32,0},{64,32},{96,64},{128,96},{160,128},{192,160},{224,192},{256... | collective-permute-start | bytes 1544 | tf_op jit(solution)/shard_map/ppermute | solution.py:568
  131.0 0.0 collective-permute-done.1.rim_offset_ref
  131.0 0.0 collective-permute-done.3.shallow_ref
  131.0 0.0 collective-permute-done.4.rim_ref
  131.0 0.0 collective-permute-done.2.top_ref
  131.0 2.6 %shard_map.59.edge_ref = f32[2,2,32]{2,1,0:T(2,128)S(1)} custom-call(f32[2,32]{1,0:T(2,128)S(1)} %collective-permute-done.offset_ref, f32[2,32]{1,0:T(2,128)S(1)} %collective-permute-done.1.rim_offset_ref, bf16[17,32,128]{2,1,0:T(8,128)(2,1)S(1)} %collective-permute-done.2.top_ref, bf16[32,32,128]{2,1,0:T(8,128)(2,1)S(1)} %collective-permute-done.3.shallow_ref, ...), custom_call_target="tpu_custom_call" | custom-call | flops 6000000 | bytes 3000000 | tf_op jit(solution)/shard_map/pallas_call | solution.py:498
  133.6 5.1 %collective-permute-done.9.middle_ref = f32[2,2,32]{2,1,0:T(2,128)S(1)} collective-permute-done((f32[2,2,32]{2,1,0:T(2,128)S(1)}, f32[2,2,32]{2,1,0:T(2,128)S(1)}, u32[]{:S(2)}, u32[]{:S(2)}) %collective-permute-start.9) | collective-permute-done | bytes 544 | tf_op jit(solution)/shard_map/ppermute | solution.py:568
  138.8 0.6 shard_map.62
  (1 shorter events, 0.0 us)
Async XLA Ops:
  0.6 0.7 copy-start.3
  2.1 17.5 %all-to-all-start = ((s32[32,1,2]{2,1,0:T(1,128)}), s32[32,1,2]{2,1,0:T(1,128)S(1)}, u32[]{:S(2)}, u32[]{:S(2)}) async-start(s32[32,1,2]{2,1,0:T(1,128)} %get-tuple-element.17), calls=%async_computation | async-start | bytes 32768 | tf_op jit(solution)/shard_map/all_to_all | solution.py:542
  11.4 1.2 copy-start.1
  12.8 8.7 %copy-start = (bf16[32,128,128]{2,1,0:T(8,128)(2,1)}, bf16[32,128,128]{2,1,0:T(8,128)(2,1)S(1)}, u32[]{:S(2)}) copy-start(bf16[32,128,128]{2,1,0:T(8,128)(2,1)S(1)} %shard_map.51.blocks_ref) | copy-start | bytes 3145732
  21.5 44.4 %all-to-all-start.1 = ((bf16[64,96,128]{2,1,0:T(8,128)(2,1)}), bf16[64,96,128]{2,1,0:T(8,128)(2,1)S(1)}, u32[]{:S(2)}, u32[]{:S(2)}) async-start(bf16[64,96,128]{2,1,0:T(8,128)(2,1)} %shard_map.52), calls=%async_computation.1 | async-start | bytes 3145728 | tf_op jit(solution)/shard_map/all_to_all | solution.py:551
  65.9 21.9 %all-to-all-start.2 = ((bf16[64,32,128]{2,1,0:T(8,128)(2,1)}), bf16[64,32,128]{2,1,0:T(8,128)(2,1)S(1)}, u32[]{:S(2)}, u32[]{:S(2)}) async-start(bf16[64,32,128]{2,1,0:T(8,128)(2,1)} %shard_map.53), calls=%async_computation.2 | async-start | bytes 1048576 | tf_op jit(solution)/shard_map/all_to_all | solution.py:553
  70.4 25.1 %copy-start.2 = (f32[1,2,32]{2,1,0:T(2,128)S(1)}, f32[1,2,32]{2,1,0:T(2,128)}, u32[]{:S(2)}) copy-start(f32[1,2,32]{2,1,0:T(2,128)} %param.5) | copy-start | bytes 772
  70.5 50.9 %collective-permute-start.8 = (bf16[33,64,128]{2,1,0:T(8,128)(2,1)S(1)}, bf16[33,64,128]{2,1,0:T(8,128)(2,1)S(1)}, u32[]{:S(2)}, u32[]{:S(2)}) collective-permute-start(bf16[33,64,128]{2,1,0:T(8,128)(2,1)S(1)} %shard_map.60), channel_id=1, source_target_pairs={{0,32},{32,64},{64,96},{96,128},{128,160},{160,192},{192,224},{224... | collective-permute-start | bytes 1622024 | tf_op jit(solution)/shard_map/ppermute | solution.py:556
  88.4 42.6 %collective-permute-start.3 = (bf16[32,32,128]{2,1,0:T(8,128)(2,1)S(1)}, bf16[32,32,128]{2,1,0:T(8,128)(2,1)S(1)}, u32[]{:S(2)}, u32[]{:S(2)}) collective-permute-start(bf16[32,32,128]{2,1,0:T(8,128)(2,1)S(1)} %shard_map.57), channel_id=1, source_target_pairs={{32,0},{64,32},{96,64},{128,96},{160,128},{192,160},{224,192},{256... | collective-permute-start | bytes 786440 | tf_op jit(solution)/shard_map/ppermute | solution.py:563
  91.8 39.2 %collective-permute-start.2 = (bf16[17,32,128]{2,1,0:T(8,128)(2,1)S(1)}, bf16[17,32,128]{2,1,0:T(8,128)(2,1)S(1)}, u32[]{:S(2)}, u32[]{:S(2)}) collective-permute-start(bf16[17,32,128]{2,1,0:T(8,128)(2,1)S(1)} %get-tuple-element.19), channel_id=1, source_target_pairs={{32,0},{64,32},{96,64},{128,96},{160,128},{192,160},{224,192},{256... | collective-permute-start | bytes 417800 | tf_op jit(solution)/shard_map/ppermute | solution.py:560
  94.2 12.6 %collective-permute-start.6 = (bf16[16,32,128]{2,1,0:T(8,128)(2,1)S(1)}, bf16[16,32,128]{2,1,0:T(8,128)(2,1)S(1)}, u32[]{:S(2)}, u32[]{:S(2)}) collective-permute-start(bf16[16,32,128]{2,1,0:T(8,128)(2,1)S(1)} %get-tuple-element.20), channel_id=1, source_target_pairs={{0,1},{1,2},{2,3},{3,4},{4,5},{5,6},{6,7},{7,8},{8,9},{9,10},{10,1... | collective-permute-start | bytes 393224 | tf_op jit(solution)/shard_map/ppermute | solution.py:558
  95.5 4.9 %collective-permute-start.5 = (f32[2,32]{1,0:T(2,128)S(1)}, f32[2,32]{1,0:T(2,128)S(1)}, u32[]{:S(2)}, u32[]{:S(2)}) collective-permute-start(f32[2,32]{1,0:T(2,128)S(1)} %bitcast.10), channel_id=1, source_target_pairs={{0,1},{1,2},{2,3},{3,4},{4,5},{5,6},{6,7},{7,8},{8,9},{9,10},{10,1... | collective-permute-start | bytes 776 | tf_op jit(solution)/shard_map/ppermute | solution.py:547
  100.4 30.6 %collective-permute-start.4 = (bf16[16,32,128]{2,1,0:T(8,128)(2,1)S(1)}, bf16[16,32,128]{2,1,0:T(8,128)(2,1)S(1)}, u32[]{:S(2)}, u32[]{:S(2)}) collective-permute-start(bf16[16,32,128]{2,1,0:T(8,128)(2,1)S(1)} %get-tuple-element.20), channel_id=1, source_target_pairs={{32,1},{33,2},{34,3},{35,4},{36,5},{37,6},{38,7},{39,8},{40,9},{41... | collective-permute-start | bytes 393224 | tf_op jit(solution)/shard_map/ppermute | solution.py:559
  106.8 12.6 %collective-permute-start.7 = (f32[2,32]{1,0:T(2,128)S(1)}, f32[2,32]{1,0:T(2,128)S(1)}, u32[]{:S(2)}, u32[]{:S(2)}) collective-permute-start(f32[2,32]{1,0:T(2,128)S(1)} %bitcast.12), channel_id=1, source_target_pairs={{0,32},{32,64},{64,96},{96,128},{128,160},{160,192},{192,224},{224... | collective-permute-start | bytes 776 | tf_op jit(solution)/shard_map/ppermute | solution.py:546
  119.4 9.7 %collective-permute-start = (f32[2,32]{1,0:T(2,128)S(1)}, f32[2,32]{1,0:T(2,128)S(1)}, u32[]{:S(2)}, u32[]{:S(2)}) collective-permute-start(f32[2,32]{1,0:T(2,128)S(1)} %bitcast.13), channel_id=1, source_target_pairs={{32,0},{64,32},{96,64},{128,96},{160,128},{192,160},{224,192},{256... | collective-permute-start | bytes 776 | tf_op jit(solution)/shard_map/ppermute | solution.py:545
  121.3 9.7 %collective-permute-start.1 = (f32[2,32]{1,0:T(2,128)S(1)}, f32[2,32]{1,0:T(2,128)S(1)}, u32[]{:S(2)}, u32[]{:S(2)}) collective-permute-start(f32[2,32]{1,0:T(2,128)S(1)} %bitcast.14), channel_id=1, source_target_pairs={{32,1},{33,2},{34,3},{35,4},{36,5},{37,6},{38,7},{39,8},{40,9},{41... | collective-permute-start | bytes 776 | tf_op jit(solution)/shard_map/ppermute | solution.py:548
  129.1 9.7 %collective-permute-start.9 = (f32[2,2,32]{2,1,0:T(2,128)S(1)}, f32[2,2,32]{2,1,0:T(2,128)S(1)}, u32[]{:S(2)}, u32[]{:S(2)}) collective-permute-start(f32[2,2,32]{2,1,0:T(2,128)S(1)} %shard_map.61), channel_id=1, source_target_pairs={{32,0},{64,32},{96,64},{128,96},{160,128},{192,160},{224,192},{256... | collective-permute-start | bytes 1544 | tf_op jit(solution)/shard_map/ppermute | solution.py:568
